TPU v7x, 512 devices: a whole 4x8x8 slice. The times are simulated.
512 devices in a mesh: grp: 8 (over z), own: 64 (over y, x, core).
Axes of the slice: x: 4, y: 8, z: 8, core: 2. Of those that a mesh axis runs over, the one named last changes fastest.
Arguments:
- amps: bfloat16 [14336, 128, 128], P(('grp', 'own')), may hold values from -0.35 to 0.35, as said below
- ints: bfloat16 [14336, 128, 128], P(('grp', 'own')), may hold values from -0.5 to 0.5, as said below
- pno_energy: float32 [14336, 128], P(('grp', 'own')), may hold values from 0.2 to 2, as said below
- occ_energy: float32 [1000], replicated, may hold values from -1 to -0.2
- pair_occ: int32 [2, 14336], P(None, ('grp', 'own')), may hold values from 0 to 999, as said below
- mirror: int32 [14336], P(('grp', 'own')), may hold values from 0 to 14335, as said below
- edge_src: int32 [24576], P(('grp', 'own')), may hold values from 0 to 14335, as said below
- edge_dst: int32 [24576], P('grp'), may hold values from 0 to 14335, as said below
- edge_fock: float32 [24576], P(('grp', 'own')), may hold values from -6 to 6
- margin: bfloat16 [24576, 128, 128], P(('grp', 'own')), may hold values from -0.15 to 1.15
Outputs:
- residual: bfloat16 [14336, 128, 128], P(('grp', 'own'))
Inputs may be any that keep to these rules, and one draw needn't show every extreme that they name: `pair_occ`: each pair's two indices differ. The pair at mirror[p] has its two indices swapped. mirror is an involution without fixed points; a pair and its mirror lie in the same grp block of pairs but never on the same device; amps and ints of mirror[p] are the transposes of those of p, and pno_energy is equal. Of one device's pairs at most 1 have their mirror on any one other device, and that many do for some device. `edge_src`: every edge of a device has its source pair on that same device. `edge_dst`: an edge's target pair lies in the same group as its source, on another device; of one device's edges at most 1 end on pairs of any one other device, and at most 1 have the mirror of their target pair on any one device (that device itself included); both bounds are reached on some device. `amps`: mirror pairs hold transposed tiles. `ints`: mirror pairs hold transposed tiles. `pno_energy`: mirror pairs hold equal rows.
All inputs are finite; a program needn't handle non-finite values.
Results may differ from a plain program's by a relative error of at most 0.0065.
Values may be sent and summed in bfloat16 or wider, within the bound.
No kernel may reach another device: no remote copies, remote signals or barrier semaphores. Data moves between devices by JAX's collectives and lax.ppermute only.
A program may use at most 64 MiB of HBM per device.

v0:
```python
import jax
import jax.numpy as jnp
from jax import lax
from jax.sharding import PartitionSpec as P


def rank_within(targets, buckets):
    onehot = (targets[:, None] == lax.iota(jnp.int32, buckets)[None, :]).astype(jnp.int32)
    running = jnp.cumsum(onehot, axis=0)
    return jnp.sum(onehot * running, axis=1) - 1


def pick_rows(lookup, hit_mask):
    return jnp.sum(jnp.where(hit_mask, lookup[None, :], 0.0), axis=1)


def pack_tiles(tile_set, targets, owners, capacity):
    placed = targets * capacity + rank_within(targets, owners)
    blank_buffer = jnp.zeros((owners * capacity,) + tile_set.shape[1:], tile_set.dtype)
    return blank_buffer.at[placed].set(tile_set)


def arrival_sum(arrived, destination, row_ids, row_total, owners, capacity, my_owner):
    per_sender = destination.shape[0] // owners
    arriving = destination == my_owner
    sender = lax.iota(jnp.int32, owners * per_sender) // per_sender
    counted = (
        jnp.cumsum(arriving.reshape(owners, per_sender).astype(jnp.int32), axis=1).reshape(-1) - 1
    )
    column = sender * capacity + counted
    row_hit = (
        (row_ids[:, None] == lax.iota(jnp.int32, row_total)[None, :]) & arriving[:, None]
    ).astype(jnp.float32)
    column_hit = (column[:, None] == lax.iota(jnp.int32, owners * capacity)[None, :]).astype(
        jnp.float32
    )
    selector = jnp.dot(row_hit.T, column_hit).astype(jnp.bfloat16)
    tile_rows = arrived.shape[1]
    tile_cols = arrived.shape[2]
    summed = jnp.dot(
        selector,
        arrived.reshape(owners * capacity, tile_rows * tile_cols),
        preferred_element_type=jnp.float32,
    )
    return summed.reshape(row_total, tile_rows, tile_cols)


def local(
    amps, ints, pno_energy, occ_energy, pair_occ, mirror, edge_src, edge_dst, edge_fock, margin
):
    owners = lax.axis_size("own")
    my_owner = lax.axis_index("own")
    group_index = lax.axis_index("grp")
    per_device = amps.shape[0]
    pno_rank = amps.shape[1]
    edge_count = edge_src.shape[0]
    occ_count = occ_energy.shape[0]
    mirror_cap = (per_device + owners - 2) // (owners - 1)
    edge_cap = (edge_count + owners - 2) // (owners - 1)
    group_base = group_index * (owners * per_device)
    device_base = group_base + my_owner * per_device
    amp_f32 = amps.astype(jnp.float32)
    int_f32 = ints.astype(jnp.float32)
    pair_energy = jnp.sum((2.0 * int_f32 - jnp.swapaxes(int_f32, 1, 2)) * amp_f32, axis=(1, 2))
    occ_ids = lax.iota(jnp.int32, occ_count)
    first_hit = pair_occ[0][:, None] == occ_ids[None, :]
    second_hit = pair_occ[1][:, None] == occ_ids[None, :]
    partial_value = jnp.sum(jnp.where(first_hit, pair_energy[:, None], 0.0), axis=0)
    source_local = edge_src - device_base
    source_tiles = jnp.take(amps, source_local, axis=0)
    projected = jnp.einsum(
        "eab,ebc->eac", margin, source_tiles, preferred_element_type=jnp.float32
    ).astype(jnp.bfloat16)
    product = jnp.einsum("eab,ecb->eac", projected, margin, preferred_element_type=jnp.float32)
    coupled = (product * edge_fock[:, None, None]).astype(jnp.bfloat16)
    group_dst = edge_dst - group_base
    dst_owner = group_dst // per_device
    dst_slot = group_dst % per_device
    my_dst_owner = lax.dynamic_slice_in_dim(dst_owner, my_owner * edge_count, edge_count)
    mirror_local = mirror - group_base
    mirror_owner = mirror_local // per_device
    mirror_slot = mirror_local % per_device
    slot_ids = lax.iota(jnp.int32, per_device)
    same_owner = mirror_owner[:, None] == mirror_owner[None, :]
    out_rank = jnp.sum(same_owner & (slot_ids[None, :] < slot_ids[:, None]), axis=1)
    in_rank = jnp.sum(same_owner & (mirror_slot[None, :] < mirror_slot[:, None]), axis=1)
    out_place = mirror_owner * mirror_cap + out_rank
    in_place = mirror_owner * mirror_cap + in_rank
    outgoing = pack_tiles(coupled, my_dst_owner, owners, edge_cap)
    arrived = lax.all_to_all(outgoing, "own", split_axis=0, concat_axis=0, tiled=True)
    coupling = arrival_sum(arrived, dst_owner, dst_slot, per_device, owners, edge_cap, my_owner)
    occ_sums = lax.psum(partial_value, ("grp", "own"))
    cepa_shift = 0.5 * (pick_rows(occ_sums, first_hit) + pick_rows(occ_sums, second_hit))
    fock_pair = pick_rows(occ_energy, first_hit) + pick_rows(occ_energy, second_hit)
    diagonal = (
        pno_energy[:, :, None]
        + pno_energy[:, None, :]
        - fock_pair[:, None, None]
        - cepa_shift[:, None, None]
    )
    local_part = 0.5 * int_f32 + diagonal * amp_f32
    half_res = (local_part + coupling).astype(jnp.bfloat16)
    sent_tiles = (
        jnp.zeros((owners * mirror_cap, pno_rank, pno_rank), jnp.bfloat16)
        .at[out_place]
        .set(half_res)
    )
    returned = lax.all_to_all(sent_tiles, "own", split_axis=0, concat_axis=0, tiled=True)
    partner_tiles = jnp.swapaxes(jnp.take(returned, in_place, axis=0), 1, 2)
    return (half_res.astype(jnp.float32) + partner_tiles.astype(jnp.float32)).astype(jnp.bfloat16)


def solution(mesh):
    in_specs = (
        P(("grp", "own"), None, None),
        P(("grp", "own"), None, None),
        P(("grp", "own"), None),
        P(),
        P(None, ("grp", "own")),
        P(("grp", "own")),
        P(("grp", "own")),
        P("grp"),
        P(("grp", "own")),
        P(("grp", "own"), None, None),
    )
    out_specs = P(("grp", "own"), None, None)
    return jax.shard_map(local, mesh=mesh, in_specs=in_specs, out_specs=out_specs, check_vma=False)
```

profile of v0, /device:TPU:1, one launch (start us, length us, event | category | flops | bytes accessed | tf_op | source)
XLA Modules:
  0.0 255.2 jit_solution(17630321323486701804)
XLA Ops:
  0.0 0.8 fusion.33
  0.9 0.1 dynamic_slice.3
  0.9 0.1 fusion.25
  1.0 0.1 reduce_window_sum.23
  1.1 0.2 select_reduce_fusion.5
  1.3 0.1 compare_select_fusion.3
  1.4 0.7 compare_and_fusion.3
  2.0 3.1 %gather_fusion = bf16[48,128,128]{2,1,0:T(8,128)(2,1)} fusion(bf16[28,128,128]{2,1,0:T(8,128)(2,1)} %param.10, s32[1024]{0:T(1024)S(1)} %pad_clamp_fusion.1), kind=kCustom, calls=%fused_computation | custom fusion | bytes 3145920 | tf_op jit(solution)/shard_map/jit(_take)/gather | solution.py:70
  5.2 3.7 %multiply_convert_fusion = bf16[48,128,128]{2,1,0:T(8,128)(2,1)S(1)} fusion(bf16[48,128,128]{2,1,0:T(8,128)(2,1)S(1)} %copy-done, f32[48]{0:T(128)S(1)} %copy-done.8, bf16[48,128,128]{2,1,0:T(8,128)(2,1)} %gather_fusion, pred[48]{0:T(512)(128)(4,1)S(1)} %get-tuple-element.18), kind=kOutput, calls=%fused_computation.4 | convolution fusion | flops 405798912 | bytes 4718832 | tf_op jit(solution)/shard_map/eab,ecb->eac/dot_general | solution.py:74
  8.9 1.8 broadcast.97.clone
  10.7 6.6 %scatter_fusion = bf16[64,128,128]{2,1,0:T(8,128)(2,1)} fusion(bf16[64,128,128]{2,1,0:T(8,128)(2,1)} %broadcast.97.clone, s32[48]{0:T(128)S(1)} %compare_select_fusion.3, bf16[48,128,128]{2,1,0:T(8,128)(2,1)S(1)} %multiply_convert_fusion), kind=kCustom, calls=%fused_computation.2 | custom fusion | bytes 4718784 | tf_op jit(solution)/shard_map/scatter | solution.py:20
  17.3 11.9 %all-to-all-start = ((bf16[64,128,128]{2,1,0:T(8,128)(2,1)}), bf16[64,128,128]{2,1,0:T(8,128)(2,1)}, u32[]{:S(2)}, u32[]{:S(2)}) async-start(bf16[64,128,128]{2,1,0:T(8,128)(2,1)} %scatter_fusion), calls=%async_computation | async-start | bytes 4194304 | tf_op jit(solution)/shard_map/all_to_all | solution.py:90
  29.2 1.3 copy.39
  30.6 0.2 reduce_window_sum.22
  30.8 0.1 sub.71
  30.9 1.5 copy.37
  32.4 2.0 fusion.3
  34.5 0.1 select_reduce_fusion.2
  34.5 137.0 %psum.7 = f32[1000]{0:T(1024)S(1)} all-reduce(f32[1000]{0:T(1024)S(1)} %select_reduce_fusion.2), channel_id=1, replica_groups=mesh['grp'=8,'own'=64] {'grp','own'}, use_global_device_ids=true, to_apply=%region_4.5 | all-reduce | flops 1000 | bytes 8000 | tf_op jit(solution)/shard_map/psum | solution.py:92
  171.6 0.3 select_reduce_fusion
  171.9 0.2 convert_reduce_fusion.1
  172.1 4.9 %fusion = f32[28,128,128]{2,0,1:T(8,128)} fusion(s32[3072]{0:T(1024)S(1)} %get-tuple-element.25, s32[3072]{0:T(1024)S(1)} %get-tuple-element.24, pred[3072]{0:T(1024)(128)(4,1)S(1)} %get-tuple-element.16, bf16[8,8,128,128]{3,2,1,0:T(8,128)(2,1)} %bitcast.8), kind=kOutput, calls=%fused_computation.8 | convolution fusion | flops 70100736 | bytes 3959808 | tf_op jit(solution)/shard_map/dot_general | solution.py:40
  177.1 2.9 %copy.43 = f32[28,128,128]{1,2,0:T(8,128)} copy(f32[28,128,128]{2,0,1:T(8,128)} %fusion) | data formatting | bytes 3670016 | tf_op jit(solution)/shard_map/dot_general | solution.py:40
  180.0 3.1 %fusion.6 = bf16[28,128,128]{1,2,0:T(8,128)(2,1)} fusion(f32[28,128,128]{1,2,0:T(8,128)} %copy.43, bf16[28,128,128]{1,2,0:T(8,128)(2,1)} %copy.39, f32[28,128,128]{1,2,0:T(8,128)S(1)} %copy.37, f32[28]{0:T(128)S(1)} %add_multiply_fusion, f32[28]{0:T(128)S(1)} %add.110, f32[28,128]{1,0:T(8,128)S(1)} %copy-done.3), kind=kLoop, calls=%fused_computation.14 | loop fusion | flops 4128768 | bytes 5519584 | tf_op jit(solution)/shard_map/convert_element_type | solution.py:102
  183.1 1.6 copy.44
  184.6 1.8 broadcast.97
  186.4 4.5 %scatter_fusion.1 = bf16[64,128,128]{2,1,0:T(8,128)(2,1)} fusion(bf16[64,128,128]{2,1,0:T(8,128)(2,1)} %broadcast.97, s32[28]{0:T(128)S(1)} %compare_select_fusion, bf16[28,128,128]{2,1,0:T(8,128)(2,1)S(1)} %copy.44), kind=kCustom, calls=%fused_computation.3 | custom fusion | bytes 2752624 | tf_op jit(solution)/shard_map/scatter | solution.py:106
  191.0 8.5 %all-to-all-start.1 = ((bf16[64,128,128]{2,1,0:T(8,128)(2,1)}), bf16[64,128,128]{2,1,0:T(8,128)(2,1)}, u32[]{:S(2)}, u32[]{:S(2)}) async-start(bf16[64,128,128]{2,1,0:T(8,128)(2,1)} %scatter_fusion.1), calls=%async_computation.1 | async-start | bytes 4194304 | tf_op jit(solution)/shard_map/all_to_all | solution.py:108
  199.5 49.6 %all-to-all-done.1 = bf16[64,128,128]{2,1,0:T(8,128)(2,1)} async-done(((bf16[64,128,128]{2,1,0:T(8,128)(2,1)}), bf16[64,128,128]{2,1,0:T(8,128)(2,1)}, u32[]{:S(2)}, u32[]{:S(2)}) %all-to-all-start.1) | async-done | bytes 2097184 | tf_op jit(solution)/shard_map/all_to_all | solution.py:108
  249.1 3.2 %gather_fusion.1 = bf16[28,128,128]{2,1,0:T(8,128)(2,1)} fusion(bf16[64,128,128]{2,1,0:T(8,128)(2,1)} %all-to-all-done.1, s32[1024]{0:T(1024)S(1)} %pad_clamp_fusion), kind=kCustom, calls=%fused_computation.1 | custom fusion | bytes 1835120 | tf_op jit(solution)/shard_map/jit(_take)/gather | solution.py:109
  252.3 1.6 fusion.7
  253.9 1.3 copy.45
  (30 shorter events, 0.2 us)
Async XLA Ops:
  0.0 5.2 %copy-start = (bf16[48,128,128]{2,1,0:T(8,128)(2,1)S(1)}, bf16[48,128,128]{2,1,0:T(8,128)(2,1)}, u32[]{:S(2)}) copy-start(bf16[48,128,128]{2,1,0:T(8,128)(2,1)} %param.19) | copy-start | bytes 4718596
  0.0 5.2 %copy-start.8 = (f32[48]{0:T(128)S(1)}, f32[48]{0:T(128)}, u32[]{:S(2)}) copy-start(f32[48]{0:T(128)} %param.18) | copy-start | bytes 580
  17.3 11.9 %copy-start.2 = (bf16[28,128,128]{2,1,0:T(8,128)(2,1)S(1)}, bf16[28,128,128]{2,1,0:T(8,128)(2,1)}, u32[]{:S(2)}) copy-start(bf16[28,128,128]{2,1,0:T(8,128)(2,1)} %param.10) | copy-start | bytes 2752516
  17.3 154.8 %all-to-all-start = ((bf16[64,128,128]{2,1,0:T(8,128)(2,1)}), bf16[64,128,128]{2,1,0:T(8,128)(2,1)}, u32[]{:S(2)}, u32[]{:S(2)}) async-start(bf16[64,128,128]{2,1,0:T(8,128)(2,1)} %scatter_fusion), calls=%async_computation | async-start | bytes 4194304 | tf_op jit(solution)/shard_map/all_to_all | solution.py:90
  30.5 1.8 copy-start.6
  32.4 139.2 %copy-start.5 = (f32[1000]{0:T(1024)S(1)}, f32[1000]{0:T(1024)}, u32[]{:S(2)}) copy-start(f32[1000]{0:T(1024)} %param.13) | copy-start | bytes 12004
  32.4 139.5 %copy-start.7 = (s32[28]{0:T(128)S(1)}, s32[28]{0:T(128)}, u32[]{:S(2)}) copy-start(s32[28]{0:T(128)} %param.15) | copy-start | bytes 340
  32.4 139.7 %copy-start.4 = (s32[3072]{0:T(1024)S(1)}, s32[3072]{0:T(1024)}, u32[]{:S(2)}) copy-start(s32[3072]{0:T(1024)} %param.17) | copy-start | bytes 36868
  177.1 2.9 %copy-start.3 = (f32[28,128]{1,0:T(8,128)S(1)}, f32[28,128]{1,0:T(8,128)}, u32[]{:S(2)}) copy-start(f32[28,128]{1,0:T(8,128)} %param.12) | copy-start | bytes 43012
  191.0 58.1 %all-to-all-start.1 = ((bf16[64,128,128]{2,1,0:T(8,128)(2,1)}), bf16[64,128,128]{2,1,0:T(8,128)(2,1)}, u32[]{:S(2)}, u32[]{:S(2)}) async-start(bf16[64,128,128]{2,1,0:T(8,128)(2,1)} %scatter_fusion.1), calls=%async_computation.1 | async-start | bytes 4194304 | tf_op jit(solution)/shard_map/all_to_all | solution.py:108
  199.5 52.8 %copy-start.1 = (bf16[28,128,128]{1,2,0:T(8,128)(2,1)S(1)}, bf16[28,128,128]{1,2,0:T(8,128)(2,1)}, u32[]{:S(2)}) copy-start(bf16[28,128,128]{1,2,0:T(8,128)(2,1)} %fusion.6) | copy-start | bytes 2752516
where the time goes:
time: 257 us; the launch traced here: 255 us
  blocking collectives  137 us (53%)
  waiting for transfers between devices  49.6 us (19%)
  local copies, waits for them, and re-layouts  29.9 us (12%)
  starting transfers between devices  20.4 us (8%)
  other arithmetic  9.49 us (4%)
  matrix products  8.65 us (3%)
    psum x1, blocking collectives, local(): occ_sums = lax.psum(partial_value, ('grp', 'own'))  137 us
    all_to_all x1, waiting for transfers between devices, local(): lax.all_to_all(sent_tiles, 'own', split_axis=0, concat_axis=0, tiled=True)  49.6 us
    all_to_all x1, starting transfers between devices, local(): lax.all_to_all(outgoing, 'own', split_axis=0, concat_axis=0, tiled=True)  11.9 us
    all_to_all x1, starting transfers between devices, local(): lax.all_to_all(sent_tiles, 'own', split_axis=0, concat_axis=0, tiled=True)  8.49 us
    scatter x1, local copies, waits for them, and re-layouts, pack_tiles(): return blank_buffer.at[placed].set(tile_set)  6.59 us
  transfers between devices with their start and end apart: 2, of which 1 were waited for; matrix products, arithmetic and copies ran while one was open for 2% of the time, Pallas kernels for 0%

commit v1 on v0

v1 whole, which is shorter than its diff:
```python
import jax
import jax.numpy as jnp
from jax import lax
from jax.experimental import pallas as pl
from jax.experimental.pallas import tpu as pltpu
from jax.sharding import PartitionSpec as P

LANES = 128
F32 = jnp.float32
BF16 = jnp.bfloat16


def contract_last(left, right):
    return lax.dot_general(left, right, (((1,), (1,)), ((), ())), preferred_element_type=F32)


def project_kernel(src_ref, margin_ref, amps_ref, out_ref):
    step = pl.program_id(0)
    count = margin_ref.shape[0]
    for k in range(count):
        tile = amps_ref[src_ref[step * count + k]]
        out_ref[k] = jnp.dot(margin_ref[k], tile, preferred_element_type=F32).astype(BF16)


def energy_kernel(amps_ref, ints_ref, out_ref):
    for k in range(amps_ref.shape[0]):
        amp = amps_ref[k].astype(F32)
        integral = ints_ref[k].astype(F32)
        out_ref[k] = jnp.sum((2.0 * integral - integral.T) * amp, axis=0, keepdims=True)


def couple_kernel(table_ref, place_ref, owner_ref, fock_ref, proj_ref, margin_ref, out_ref):
    step = pl.program_id(0)
    count = margin_ref.shape[0]
    half = margin_ref.shape[1] // 2
    for k in range(count):
        e = step * count + k
        code = table_ref[place_ref[e]]
        lead = (code & 1) == 1
        other = code >> 1
        proj = proj_ref[k]
        marg = margin_ref[k]
        turned = jnp.concatenate([marg[half:], marg[:half]], axis=0)
        left = jnp.where(lead, proj, turned)
        right = jnp.where(lead, marg, proj)
        tile = (contract_last(left, right) * fock_ref[e]).astype(BF16)
        out_ref[owner_ref[e], :half, :] = tile[:half]
        out_ref[other, half:, :] = tile[half:]


def base_kernel(lead_ref, occ_ref, first_ref, second_ref, amps_ref, ints_ref, pno_ref, base_ref, amp_ref):
    step = pl.program_id(0)
    count = amps_ref.shape[0]
    half = amps_ref.shape[1] // 2
    for k in range(count):
        p = step * count + k
        fock = occ_ref[first_ref[p]] + occ_ref[second_ref[p]]
        row = jnp.broadcast_to(pno_ref[k], (2 * half, 2 * half))
        level = row + row.T - fock

        @pl.when(lead_ref[p] == 1)
        def _():
            amp = amps_ref[k][:half]
            base_ref[k] = 0.5 * ints_ref[k][:half].astype(F32) + level[:half] * amp.astype(F32)
            amp_ref[k] = amp

        @pl.when(lead_ref[p] == 0)
        def _():
            amp = amps_ref[k].astype(F32).T[half:]
            integral = ints_ref[k].astype(F32).T[half:]
            base_ref[k] = 0.5 * integral + level[half:] * amp
            amp_ref[k] = amp.astype(BF16)


def sum_kernel(direct_ref, turned_ref, target_ref, shift_ref, arrived_ref, base_ref, amp_ref, sent_ref, own_ref, direct_acc, turned_acc):
    step = pl.program_id(0)
    count = arrived_ref.shape[0]
    half = arrived_ref.shape[1] // 2
    pairs = own_ref.shape[0]

    @pl.when(step == 0)
    def _():
        direct_acc[...] = jnp.zeros_like(direct_acc)
        turned_acc[...] = jnp.zeros_like(turned_acc)

    for k in range(count):
        s = step * count + k
        direct_acc[direct_ref[s]] += arrived_ref[k, :half, :].astype(F32)
        turned_acc[turned_ref[s]] += arrived_ref[k, half:, :].astype(F32)

    @pl.when(step == pl.num_programs(0) - 1)
    def _():
        def finish(p, carry):
            local = base_ref[p] - shift_ref[p] * amp_ref[p].astype(F32)
            first = (local + direct_acc[p]).astype(BF16)
            second = (local + turned_acc[p]).astype(BF16)
            res = (first.astype(F32) + second.astype(F32)).astype(BF16)
            own_ref[p] = res
            sent_ref[target_ref[p]] = res
            return carry

        lax.fori_loop(0, pairs, finish, 0, unroll=2)


def join_kernel(lead_ref, target_ref, returned_ref, own_ref, out_ref):
    step = pl.program_id(0)
    count = out_ref.shape[0]
    half = own_ref.shape[1]
    for k in range(count):
        p = step * count + k

        @pl.when(lead_ref[p] == 1)
        def _():
            out_ref[k, :half, :] = own_ref[k]
            out_ref[k, half:, :] = returned_ref[target_ref[p]]

        @pl.when(lead_ref[p] == 0)
        def _():
            whole = jnp.concatenate([returned_ref[target_ref[p]], own_ref[k]], axis=0)
            out_ref[k] = whole.astype(F32).T.astype(BF16)


def blocks(count, *rest):
    zeros = (0,) * len(rest)
    return pl.BlockSpec((count, *rest), lambda i, *_: (i, *zeros))


def whole(*shape):
    zeros = (0,) * len(shape)
    return pl.BlockSpec(shape, lambda i, *_: zeros)


def call(kernel, name, prefetch, grid, in_specs, out_specs, out_shape, flops, nbytes, scratch=()):
    return pl.pallas_call(
        kernel,
        grid_spec=pltpu.PrefetchScalarGridSpec(
            num_scalar_prefetch=prefetch,
            grid=(grid,),
            in_specs=in_specs,
            out_specs=out_specs,
            scratch_shapes=scratch,
        ),
        out_shape=out_shape,
        name=name,
        cost_estimate=pl.CostEstimate(flops=flops, bytes_accessed=nbytes, transcendentals=0),
        compiler_params=pltpu.CompilerParams(dimension_semantics=("arbitrary",)),
    )


def pick_rows(lookup, hit_mask):
    return jnp.sum(jnp.where(hit_mask, lookup[None, :], 0.0), axis=1)


def all_sum(value, axis, size):
    step = 1
    while step < size:
        value = value + lax.ppermute(value, axis, [(i, i ^ step) for i in range(size)])
        step *= 2
    return value


def exchange(tiles):
    return lax.all_to_all(tiles, "own", split_axis=0, concat_axis=0, tiled=True)


def local(
    amps, ints, pno_energy, occ_energy, pair_occ, mirror, edge_src, edge_dst, edge_fock, margin
):
    owners = lax.axis_size("own")
    groups = lax.axis_size("grp")
    my_owner = lax.axis_index("own")
    group_index = lax.axis_index("grp")
    pairs, rank, _ = amps.shape
    half = rank // 2
    edges = edge_src.shape[0]
    occ_count = occ_energy.shape[0]
    group_base = group_index * (owners * pairs)
    device_base = group_base + my_owner * pairs
    tile_bytes = rank * rank * 2

    ids = device_base + lax.iota(jnp.int32, pairs)
    lead = (ids < mirror).astype(jnp.int32)
    mirror_owner = (mirror - group_base) // pairs
    code = jnp.pad(mirror_owner * 2 + lead, (0, LANES - pairs))
    codes = exchange(jnp.broadcast_to(code[None, None, :], (owners, 1, LANES)))
    table = codes.reshape(owners * LANES)

    edge_step = 8
    projected = call(
        project_kernel,
        "project",
        1,
        edges // edge_step,
        [blocks(edge_step, rank, rank), whole(pairs, rank, rank)],
        blocks(edge_step, rank, rank),
        jax.ShapeDtypeStruct((edges, rank, rank), BF16),
        2 * edges * rank**3,
        (2 * edges + pairs) * tile_bytes,
    )(edge_src - device_base, margin, amps)

    pair_step = 4
    lane_energy = call(
        energy_kernel,
        "energy",
        0,
        pairs // pair_step,
        [blocks(pair_step, rank, rank), blocks(pair_step, rank, rank)],
        blocks(pair_step, 1, rank),
        jax.ShapeDtypeStruct((pairs, 1, rank), F32),
        6 * pairs * rank**2,
        2 * pairs * tile_bytes,
    )(amps, ints)
    pair_energy = jnp.sum(lane_energy, axis=(1, 2))
    padded = -(-occ_count // LANES) * LANES
    occ_ids = lax.iota(jnp.int32, padded)
    first_hit = pair_occ[0][:, None] == occ_ids[None, :]
    second_hit = pair_occ[1][:, None] == occ_ids[None, :]
    partial_value = jnp.sum(jnp.where(first_hit, pair_energy[:, None], 0.0), axis=0)

    group_dst = edge_dst - group_base
    dst_owner = group_dst // pairs
    dst_slot = group_dst % pairs
    my_owner_row = lax.dynamic_slice_in_dim(dst_owner, my_owner * edges, edges)
    my_slot_row = lax.dynamic_slice_in_dim(dst_slot, my_owner * edges, edges)
    outgoing = call(
        couple_kernel,
        "couple",
        4,
        edges // edge_step,
        [blocks(edge_step, rank, rank), blocks(edge_step, rank, rank)],
        whole(owners, rank, rank),
        jax.ShapeDtypeStruct((owners, rank, rank), BF16),
        2 * edges * rank**3,
        (2 * edges + owners) * tile_bytes,
    )(table, my_owner_row * LANES + my_slot_row, my_owner_row, edge_fock, projected, margin)
    arrived = exchange(outgoing)

    total = partial_value.reshape(padded // LANES, LANES)
    total = all_sum(total, "grp", groups)
    total = all_sum(total, "own", owners)
    occ_sums = total.reshape(padded)
    shift = 0.5 * (pick_rows(occ_sums, first_hit) + pick_rows(occ_sums, second_hit))
    base, amp_half = call(
        base_kernel,
        "base",
        4,
        pairs // pair_step,
        [blocks(pair_step, rank, rank), blocks(pair_step, rank, rank), blocks(pair_step, 1, rank)],
        [blocks(pair_step, half, rank), blocks(pair_step, half, rank)],
        [
            jax.ShapeDtypeStruct((pairs, half, rank), F32),
            jax.ShapeDtypeStruct((pairs, half, rank), BF16),
        ],
        6 * pairs * rank**2,
        4 * pairs * tile_bytes,
    )(lead, occ_energy, pair_occ[0], pair_occ[1], amps, ints, pno_energy.reshape(pairs, 1, rank))
    by_sender = group_dst.reshape(owners, edges)
    direct_hit = by_sender // pairs == my_owner
    direct_row = jnp.max(jnp.where(direct_hit, by_sender % pairs + 1, 0), axis=1)
    mirror_local = mirror - group_base
    turned_hit = by_sender[:, :, None] == mirror_local[None, None, :]
    turned_row = jnp.max(
        jnp.where(turned_hit, lax.iota(jnp.int32, pairs)[None, None, :] + 1, 0), axis=(1, 2)
    )
    direct_row = jnp.where(direct_row == 0, pairs, direct_row - 1)
    turned_row = jnp.where(turned_row == 0, pairs, turned_row - 1)

    owner_step = 8
    sent, own_half = call(
        sum_kernel,
        "sum",
        4,
        owners // owner_step,
        [
            blocks(owner_step, rank, rank),
            whole(pairs, half, rank),
            whole(pairs, half, rank),
        ],
        [whole(owners, half, rank), whole(pairs, half, rank)],
        [
            jax.ShapeDtypeStruct((owners, half, rank), BF16),
            jax.ShapeDtypeStruct((pairs, half, rank), BF16),
        ],
        4 * owners * rank**2,
        (2 * owners + 2 * pairs) * tile_bytes,
        [pltpu.VMEM((pairs + 1, half, rank), F32), pltpu.VMEM((pairs + 1, half, rank), F32)],
    )(direct_row, turned_row, mirror_owner, shift, arrived, base, amp_half)
    returned = exchange(sent)
    return call(
        join_kernel,
        "join",
        2,
        pairs // pair_step,
        [whole(owners, half, rank), blocks(pair_step, half, rank)],
        blocks(pair_step, rank, rank),
        jax.ShapeDtypeStruct((pairs, rank, rank), BF16),
        pairs * rank**2,
        (owners // 2 + 2 * pairs) * tile_bytes,
    )(lead, mirror_owner, returned, own_half)


def solution(mesh):
    in_specs = (
        P(("grp", "own"), None, None),
        P(("grp", "own"), None, None),
        P(("grp", "own"), None),
        P(),
        P(None, ("grp", "own")),
        P(("grp", "own")),
        P(("grp", "own")),
        P("grp"),
        P(("grp", "own")),
        P(("grp", "own"), None, None),
    )
    out_specs = P(("grp", "own"), None, None)
    return jax.shard_map(local, mesh=mesh, in_specs=in_specs, out_specs=out_specs, check_vma=False)
```

time: 257 us -> 167 us (0.65)
  blocking collectives: 137 us -> 39.2 us
  starting transfers between devices: 20.4 us -> 66.3 us
  waiting for transfers between devices: 49.6 us -> 9.71 us
  Pallas kernels: 0 us -> 38.1 us
  local copies, waits for them, and re-layouts: 29.9 us -> 3.96 us
  matrix products: 8.65 us -> 0 us
    psum x1 -> x0, blocking collectives: 137 us -> none  [local(): occ_sums = lax.psum(partial_value, ('grp', 'own'))]
    all_to_all x2, waiting for transfers between devices: 49.6 us -> 0.66 us  [exchange(): return lax.all_to_all(tiles, 'own', split_axis=0, concat_axis=0, tiled=True)]
    ppermute x0 -> x9, starting transfers between devices: none -> 44.9 us  [all_sum(): lax.ppermute(value, axis, [(i, i ^ step) for i in range(size)])]
    all_to_all x0 -> x1, blocking collectives: none -> 39.2 us  [exchange(): return lax.all_to_all(tiles, 'own', split_axis=0, concat_axis=0, tiled=True)]
    pallas_call x0 -> x6, Pallas kernels: none -> 38.1 us  [the longest x1 7.31 us: local(): call(base_kernel, 'base', 4, pairs // pair_step, [blocks(pair_step, rank,...]
    scatter x2 -> x0, local copies, waits for them, and re-layouts: 11.1 us -> none  [the longest x1 6.59 us: pack_tiles(): return blank_buffer.at[placed].set(tile_set)]
    ppermute x0 -> x9, waiting for transfers between devices: none -> 9.05 us  [all_sum(): lax.ppermute(value, axis, [(i, i ^ step) for i in range(size)])]
    dot_general x2 -> x0, matrix products: 8.65 us -> none  [the longest x1 4.92 us: arrival_sum(): jnp.dot(selector, arrived.reshape(owners * capacity, tile_rows * tile_col...]
  transfers between devices with their start and end apart: 2 -> 11, of which waited for: 1 -> 9; matrix products, arithmetic and copies ran while one was open for 2% -> 5% of each run, Pallas kernels for 0% -> 11%
where the time goes in v1:
time: 167 us; the launch traced here: 165 us
  starting transfers between devices  66.3 us (40%)
  blocking collectives  39.2 us (23%)
  Pallas kernels  38.1 us (23%)
  waiting for transfers between devices  9.71 us (6%)
  other arithmetic  7.77 us (5%)
  local copies, waits for them, and re-layouts  3.96 us (2%)
    ppermute x9, starting transfers between devices, all_sum(): lax.ppermute(value, axis, [(i, i ^ step) for i in range(size)])  44.9 us
    all_to_all x1, blocking collectives, exchange(): return lax.all_to_all(tiles, 'own', split_axis=0, concat_axis=0, tiled=True)  39.2 us
    all_to_all x2, starting transfers between devices, exchange(): return lax.all_to_all(tiles, 'own', split_axis=0, concat_axis=0, tiled=True)  21.4 us
    ppermute x9, waiting for transfers between devices, all_sum(): lax.ppermute(value, axis, [(i, i ^ step) for i in range(size)])  9.05 us
    pallas_call x1, Pallas kernels, local(): call(base_kernel, 'base', 4, pairs // pair_step, [blocks(pair_step, rank,...  7.31 us
    pallas_call x1, Pallas kernels, local(): call(couple_kernel, 'couple', 4, edges // edge_step, [blocks(edge_step, r...  7.02 us
    pallas_call x1, Pallas kernels, local(): call(sum_kernel, 'sum', 4, owners // owner_step, [blocks(owner_step, rank...  6.96 us
    pallas_call x1, Pallas kernels, local(): call(project_kernel, 'project', 1, edges // edge_step, [blocks(edge_step,...  6.07 us
  transfers between devices with their start and end apart: 11, of which 9 were waited for; matrix products, arithmetic and copies ran while one was open for 5% of the time, Pallas kernels for 11%

profile of v1, /device:TPU:1, one launch (start us, length us, event | category | flops | bytes accessed | tf_op | source)
XLA Modules:
  0.0 165.3 jit_solution(7759877067057696742)
XLA Ops:
  0.0 1.2 multiply_add_fusion
  1.9 11.6 %all-to-all-start = ((s32[64,1,128]{2,1,0:T(1,128)}), s32[64,1,128]{2,1,0:T(1,128)S(1)}, u32[]{:S(2)}, u32[]{:S(2)}) async-start(s32[64,1,128]{2,1,0:T(1,128)} %broadcast_in_dim.65), calls=%async_computation | async-start | bytes 65536 | tf_op jit(solution)/shard_map/all_to_all | solution.py:163
  13.5 0.7 broadcast_compare_fusion
  14.3 1.2 broadcast_subtract_fusion.1.src_ref
  16.1 6.1 %project.1.proj_ref = bf16[48,128,128]{2,1,0:T(8,128)(2,1)} custom-call(s32[48]{0:T(128)} %broadcast_subtract_fusion.1.src_ref, bf16[48,128,128]{2,1,0:T(8,128)(2,1)} %margin_ref.3, bf16[28,128,128]{2,1,0:T(8,128)(2,1)} %amps_ref.5), custom_call_target="tpu_custom_call" | custom-call | flops 201326592 | bytes 4063232 | tf_op jit(solution)/shard_map/project/pallas_call | solution.py:189
  23.5 7.0 %couple.1 = bf16[64,128,128]{2,1,0:T(8,128)(2,1)} custom-call(s32[8192]{0:T(1024)} %bitcast.11, s32[48]{0:T(128)} %get-tuple-element.15.place_ref, s32[48]{0:T(128)} %get-tuple-element.16.owner_ref, f32[48]{0:T(128)} %fock_ref.1, bf16[48,128,128]{2,1,0:T(8,128)(2,1)} %project.1.proj_ref, bf16[48,128,128]{2,1,0:T(8,128)(2,1)} %margin_ref.3), custom_call_target="tpu_custom_call" | custom-call | flops 201326592 | bytes 5242880 | tf_op jit(solution)/shard_map/couple/pallas_call | solution.py:225
  30.5 9.8 %all-to-all-start.1 = ((bf16[64,128,128]{2,1,0:T(8,128)(2,1)}), bf16[64,128,128]{2,1,0:T(8,128)(2,1)S(1)}, u32[]{:S(2)}, u32[]{:S(2)}) async-start(bf16[64,128,128]{2,1,0:T(8,128)(2,1)} %couple.1), calls=%async_computation.1 | async-start | bytes 4194304 | tf_op jit(solution)/shard_map/all_to_all | solution.py:163
  40.3 5.1 %energy.1 = f32[28,1,128]{2,1,0:T(1,128)} custom-call(bf16[28,128,128]{2,1,0:T(8,128)(2,1)} %amps_ref.5, bf16[28,128,128]{2,1,0:T(8,128)(2,1)} %ints_ref.3), custom_call_target="tpu_custom_call" | custom-call | flops 2752512 | bytes 1835008 | tf_op jit(solution)/shard_map/energy/pallas_call | solution.py:202
  45.3 1.0 reduce_sum.36
  47.0 4.0 %collective-permute-start = (f32[8,128]{1,0:T(8,128)S(1)}, f32[8,128]{1,0:T(8,128)S(1)}, u32[]{:S(2)}, u32[]{:S(2)}) collective-permute-start(f32[8,128]{1,0:T(8,128)S(1)} %bitcast.12), channel_id=1, source_target_pairs={{0,64},{64,0},{128,192},{192,128},{256,320},{320,256},{384,448},{4... | collective-permute-start | bytes 12296 | tf_op jit(solution)/shard_map/ppermute | solution.py:157
  51.0 1.3 collective-permute-done
  52.3 5.8 %collective-permute-start.1 = (f32[8,128]{1,0:T(8,128)S(1)}, f32[8,128]{1,0:T(8,128)S(1)}, u32[]{:S(2)}, u32[]{:S(2)}) collective-permute-start(f32[8,128]{1,0:T(8,128)S(1)} %bitcast_add_fusion), channel_id=1, source_target_pairs={{0,128},{64,192},{128,0},{192,64},{256,384},{320,448},{384,256},{4... | collective-permute-start | bytes 12296 | tf_op jit(solution)/shard_map/ppermute | solution.py:157
  58.1 1.3 collective-permute-done.1
  59.4 8.4 %collective-permute-start.2 = (f32[8,128]{1,0:T(8,128)S(1)}, f32[8,128]{1,0:T(8,128)S(1)}, u32[]{:S(2)}, u32[]{:S(2)}) collective-permute-start(f32[8,128]{1,0:T(8,128)S(1)} %fusion.6), channel_id=1, source_target_pairs={{0,256},{64,320},{128,384},{192,448},{256,0},{320,64},{384,128},{4... | collective-permute-start | bytes 12296 | tf_op jit(solution)/shard_map/ppermute | solution.py:157
  67.9 1.2 collective-permute-done.2
  69.1 4.7 %collective-permute-start.3 = (f32[8,128]{1,0:T(8,128)S(1)}, f32[8,128]{1,0:T(8,128)S(1)}, u32[]{:S(2)}, u32[]{:S(2)}) collective-permute-start(f32[8,128]{1,0:T(8,128)S(1)} %add.88), channel_id=1, source_target_pairs={{0,1},{1,0},{2,3},{3,2},{4,5},{5,4},{6,7},{7,6},{8,9},{9,8},{10,11... | collective-permute-start | bytes 12296 | tf_op jit(solution)/shard_map/ppermute | solution.py:157
  73.8 0.8 collective-permute-done.3
  74.6 3.2 %collective-permute-start.4 = (f32[8,128]{1,0:T(8,128)S(1)}, f32[8,128]{1,0:T(8,128)S(1)}, u32[]{:S(2)}, u32[]{:S(2)}) collective-permute-start(f32[8,128]{1,0:T(8,128)S(1)} %add.89), channel_id=1, source_target_pairs={{0,2},{1,3},{2,0},{3,1},{4,6},{5,7},{6,4},{7,5},{8,10},{9,11},{10,... | collective-permute-start | bytes 12296 | tf_op jit(solution)/shard_map/ppermute | solution.py:157
  77.9 1.3 collective-permute-done.4
  79.2 4.7 %collective-permute-start.5 = (f32[8,128]{1,0:T(8,128)S(1)}, f32[8,128]{1,0:T(8,128)S(1)}, u32[]{:S(2)}, u32[]{:S(2)}) collective-permute-start(f32[8,128]{1,0:T(8,128)S(1)} %add.90), channel_id=1, source_target_pairs={{0,4},{1,5},{2,6},{3,7},{4,0},{5,1},{6,2},{7,3},{8,12},{9,13},{10,... | collective-permute-start | bytes 12296 | tf_op jit(solution)/shard_map/ppermute | solution.py:157
  84.2 1.2 collective-permute-done.5
  85.4 3.2 %collective-permute-start.6 = (f32[8,128]{1,0:T(8,128)S(1)}, f32[8,128]{1,0:T(8,128)S(1)}, u32[]{:S(2)}, u32[]{:S(2)}) collective-permute-start(f32[8,128]{1,0:T(8,128)S(1)} %add.91), channel_id=1, source_target_pairs={{0,8},{1,9},{2,10},{3,11},{4,12},{5,13},{6,14},{7,15},{8,0},{9,1},... | collective-permute-start | bytes 12296 | tf_op jit(solution)/shard_map/ppermute | solution.py:157
  89.1 1.0 collective-permute-done.6
  90.1 4.1 %collective-permute-start.7 = (f32[8,128]{1,0:T(8,128)S(1)}, f32[8,128]{1,0:T(8,128)S(1)}, u32[]{:S(2)}, u32[]{:S(2)}) collective-permute-start(f32[8,128]{1,0:T(8,128)S(1)} %add.92), channel_id=1, source_target_pairs={{0,16},{1,17},{2,18},{3,19},{4,20},{5,21},{6,22},{7,23},{8,24},{9,... | collective-permute-start | bytes 12296 | tf_op jit(solution)/shard_map/ppermute | solution.py:157
  94.3 1.0 collective-permute-done.7
  95.3 6.9 %collective-permute-start.8 = (f32[8,128]{1,0:T(8,128)S(1)}, f32[8,128]{1,0:T(8,128)S(1)}, u32[]{:S(2)}, u32[]{:S(2)}) collective-permute-start(f32[8,128]{1,0:T(8,128)S(1)} %add.93), channel_id=1, source_target_pairs={{0,32},{1,33},{2,34},{3,35},{4,36},{5,37},{6,38},{7,39},{8,40},{9,... | collective-permute-start | bytes 12296 | tf_op jit(solution)/shard_map/ppermute | solution.py:157
  103.3 7.3 %base.1 = (f32[28,64,128]{2,1,0:T(8,128)}, bf16[28,64,128]{2,1,0:T(8,128)(2,1)}) custom-call(s32[28]{0:T(128)} %get-tuple-element.22.lead_ref, f32[1000]{0:T(1024)} %occ_ref.1, s32[28]{0:T(128)} %copy-done.3, s32[28]{0:T(128)} %get-tuple-element.24.second_ref, bf16[28,128,128]{2,1,0:T(8,128)(2,1)} %amps_ref.5, bf16[28,128,128]{2,1,0:T(8,128)(2,1)} %ints_ref.3, ...), custom_call_target="tpu_custom_call" | custom-call | flops 2752512 | bytes 3670016 | tf_op jit(solution)/shard_map/base/pallas_call | solution.py:243
  110.6 0.8 select_reduce_fusion.1
  112.0 1.3 copy-done
  113.3 7.0 %sum.1 = (bf16[64,64,128]{2,1,0:T(8,128)(2,1)}, bf16[28,64,128]{2,1,0:T(8,128)(2,1)}) custom-call(s32[64]{0:T(128)} %compare_select_fusion.1.direct_ref, s32[64]{0:T(128)} %compare_select_fusion.turned_ref, s32[28]{0:T(128)} %get-tuple-element.20.target_ref, f32[28]{0:T(128)} %add_multiply_fusion.shift_ref, bf16[64,128,128]{2,1,0:T(8,128)(2,1)} %copy-done, ...), custom_call_target="tpu_custom_call" | custom-call | flops 4194304 | bytes 6029312 | tf_op jit(solution)/shard_map/sum/pallas_call | solution.py:269
  120.3 39.2 %all_to_all.15.returned_ref = bf16[64,64,128]{2,1,0:T(8,128)(2,1)} all-to-all(bf16[64,64,128]{2,1,0:T(8,128)(2,1)} %get-tuple-element.11), channel_id=1, replica_groups=mesh['grp'=8,'own'=64] {'own'}, dimensions={0} | all-to-all | bytes 2097152 | tf_op jit(solution)/shard_map/all_to_all | solution.py:163
  159.6 5.7 %join.1 = bf16[28,128,128]{2,1,0:T(8,128)(2,1)} custom-call(s32[28]{0:T(128)} %get-tuple-element.22.lead_ref, s32[28]{0:T(128)} %get-tuple-element.20.target_ref, bf16[64,64,128]{2,1,0:T(8,128)(2,1)} %all_to_all.15.returned_ref, bf16[28,64,128]{2,1,0:T(8,128)(2,1)} %get-tuple-element.12.own_ref), custom_call_target="tpu_custom_call" | custom-call | flops 458752 | bytes 2883584 | tf_op jit(solution)/shard_map/join/pallas_call | solution.py:289
  (37 shorter events, 6.1 us)
Async XLA Ops:
  1.9 20.9 %all-to-all-start = ((s32[64,1,128]{2,1,0:T(1,128)}), s32[64,1,128]{2,1,0:T(1,128)S(1)}, u32[]{:S(2)}, u32[]{:S(2)}) async-start(s32[64,1,128]{2,1,0:T(1,128)} %broadcast_in_dim.65), calls=%async_computation | async-start | bytes 65536 | tf_op jit(solution)/shard_map/all_to_all | solution.py:163
  22.8 0.6 copy-start.1
  30.5 15.9 %copy-start.5 = (s32[2,28]{1,0:T(2,128)S(1)}, s32[2,28]{1,0:T(2,128)}, u32[]{:S(2)}) copy-start(s32[2,28]{1,0:T(2,128)} %param.14) | copy-start | bytes 676
  30.5 81.5 %all-to-all-start.1 = ((bf16[64,128,128]{2,1,0:T(8,128)(2,1)}), bf16[64,128,128]{2,1,0:T(8,128)(2,1)S(1)}, u32[]{:S(2)}, u32[]{:S(2)}) async-start(bf16[64,128,128]{2,1,0:T(8,128)(2,1)} %couple.1), calls=%async_computation.1 | async-start | bytes 4194304 | tf_op jit(solution)/shard_map/all_to_all | solution.py:163
  40.3 62.4 %copy-start.2 = (f32[28,128]{1,0:T(8,128)S(1)}, f32[28,128]{1,0:T(8,128)}, u32[]{:S(2)}) copy-start(f32[28,128]{1,0:T(8,128)} %param.12) | copy-start | bytes 43012
  46.9 56.4 %copy-start.3 = (s32[28]{0:T(128)}, s32[28]{0:T(128)S(1)}, u32[]{:S(2)}) copy-start(s32[28]{0:T(128)S(1)} %get-tuple-element.23.first_ref) | copy-start | bytes 340
  46.9 63.7 %copy-start.4 = (s32[28]{0:T(128)S(1)}, s32[28]{0:T(128)}, u32[]{:S(2)}) copy-start(s32[28]{0:T(128)} %get-tuple-element.24.second_ref) | copy-start | bytes 340
  47.0 5.3 %collective-permute-start = (f32[8,128]{1,0:T(8,128)S(1)}, f32[8,128]{1,0:T(8,128)S(1)}, u32[]{:S(2)}, u32[]{:S(2)}) collective-permute-start(f32[8,128]{1,0:T(8,128)S(1)} %bitcast.12), channel_id=1, source_target_pairs={{0,64},{64,0},{128,192},{192,128},{256,320},{320,256},{384,448},{4... | collective-permute-start | bytes 12296 | tf_op jit(solution)/shard_map/ppermute | solution.py:157
  52.3 7.1 %collective-permute-start.1 = (f32[8,128]{1,0:T(8,128)S(1)}, f32[8,128]{1,0:T(8,128)S(1)}, u32[]{:S(2)}, u32[]{:S(2)}) collective-permute-start(f32[8,128]{1,0:T(8,128)S(1)} %bitcast_add_fusion), channel_id=1, source_target_pairs={{0,128},{64,192},{128,0},{192,64},{256,384},{320,448},{384,256},{4... | collective-permute-start | bytes 12296 | tf_op jit(solution)/shard_map/ppermute | solution.py:157
  59.4 9.6 %collective-permute-start.2 = (f32[8,128]{1,0:T(8,128)S(1)}, f32[8,128]{1,0:T(8,128)S(1)}, u32[]{:S(2)}, u32[]{:S(2)}) collective-permute-start(f32[8,128]{1,0:T(8,128)S(1)} %fusion.6), channel_id=1, source_target_pairs={{0,256},{64,320},{128,384},{192,448},{256,0},{320,64},{384,128},{4... | collective-permute-start | bytes 12296 | tf_op jit(solution)/shard_map/ppermute | solution.py:157
  69.1 5.5 %collective-permute-start.3 = (f32[8,128]{1,0:T(8,128)S(1)}, f32[8,128]{1,0:T(8,128)S(1)}, u32[]{:S(2)}, u32[]{:S(2)}) collective-permute-start(f32[8,128]{1,0:T(8,128)S(1)} %add.88), channel_id=1, source_target_pairs={{0,1},{1,0},{2,3},{3,2},{4,5},{5,4},{6,7},{7,6},{8,9},{9,8},{10,11... | collective-permute-start | bytes 12296 | tf_op jit(solution)/shard_map/ppermute | solution.py:157
  74.6 4.7 %collective-permute-start.4 = (f32[8,128]{1,0:T(8,128)S(1)}, f32[8,128]{1,0:T(8,128)S(1)}, u32[]{:S(2)}, u32[]{:S(2)}) collective-permute-start(f32[8,128]{1,0:T(8,128)S(1)} %add.89), channel_id=1, source_target_pairs={{0,2},{1,3},{2,0},{3,1},{4,6},{5,7},{6,4},{7,5},{8,10},{9,11},{10,... | collective-permute-start | bytes 12296 | tf_op jit(solution)/shard_map/ppermute | solution.py:157
  79.2 6.2 %collective-permute-start.5 = (f32[8,128]{1,0:T(8,128)S(1)}, f32[8,128]{1,0:T(8,128)S(1)}, u32[]{:S(2)}, u32[]{:S(2)}) collective-permute-start(f32[8,128]{1,0:T(8,128)S(1)} %add.90), channel_id=1, source_target_pairs={{0,4},{1,5},{2,6},{3,7},{4,0},{5,1},{6,2},{7,3},{8,12},{9,13},{10,... | collective-permute-start | bytes 12296 | tf_op jit(solution)/shard_map/ppermute | solution.py:157
  85.4 4.6 %collective-permute-start.6 = (f32[8,128]{1,0:T(8,128)S(1)}, f32[8,128]{1,0:T(8,128)S(1)}, u32[]{:S(2)}, u32[]{:S(2)}) collective-permute-start(f32[8,128]{1,0:T(8,128)S(1)} %add.91), channel_id=1, source_target_pairs={{0,8},{1,9},{2,10},{3,11},{4,12},{5,13},{6,14},{7,15},{8,0},{9,1},... | collective-permute-start | bytes 12296 | tf_op jit(solution)/shard_map/ppermute | solution.py:157
  90.1 5.2 %collective-permute-start.7 = (f32[8,128]{1,0:T(8,128)S(1)}, f32[8,128]{1,0:T(8,128)S(1)}, u32[]{:S(2)}, u32[]{:S(2)}) collective-permute-start(f32[8,128]{1,0:T(8,128)S(1)} %add.92), channel_id=1, source_target_pairs={{0,16},{1,17},{2,18},{3,19},{4,20},{5,21},{6,22},{7,23},{8,24},{9,... | collective-permute-start | bytes 12296 | tf_op jit(solution)/shard_map/ppermute | solution.py:157
  95.3 15.3 %collective-permute-start.8 = (f32[8,128]{1,0:T(8,128)S(1)}, f32[8,128]{1,0:T(8,128)S(1)}, u32[]{:S(2)}, u32[]{:S(2)}) collective-permute-start(f32[8,128]{1,0:T(8,128)S(1)} %add.93), channel_id=1, source_target_pairs={{0,32},{1,33},{2,34},{3,35},{4,36},{5,37},{6,38},{7,39},{8,40},{9,... | collective-permute-start | bytes 12296 | tf_op jit(solution)/shard_map/ppermute | solution.py:157
  112.0 1.3 copy-start

commit v2 on v0

v2 whole, which is shorter than its diff:
```python
import jax
import jax.numpy as jnp
from jax import lax
from jax.experimental import pallas as pl
from jax.experimental.pallas import tpu as pltpu
from jax.sharding import PartitionSpec as P

LANES = 128
F32 = jnp.float32
BF16 = jnp.bfloat16
KERNEL_VMEM = 16 * 2**20


def contract_last(left, right):
    return lax.dot_general(left, right, (((1,), (1,)), ((), ())), preferred_element_type=F32)


def project_kernel(src_ref, margin_ref, amps_ref, out_ref):
    def body(e, carry):
        tile = amps_ref[src_ref[e]]
        out_ref[e] = jnp.dot(margin_ref[e], tile, preferred_element_type=F32).astype(BF16)
        return carry

    lax.fori_loop(0, margin_ref.shape[0], body, 0, unroll=8)


def energy_kernel(amps_ref, ints_ref, out_ref):
    def body(p, carry):
        amp = amps_ref[p].astype(F32)
        integral = ints_ref[p].astype(F32)
        out_ref[p] = jnp.sum((2.0 * integral - integral.T) * amp, axis=0, keepdims=True)
        return carry

    lax.fori_loop(0, amps_ref.shape[0], body, 0, unroll=4)


def couple_kernel(table_ref, place_ref, owner_ref, fock_ref, proj_ref, margin_ref, out_ref, tiles, sems):
    half = margin_ref.shape[1] // 2
    edges = margin_ref.shape[0]

    def copies(e, other):
        direct = pltpu.make_async_copy(
            tiles.at[e, pl.ds(0, half)], out_ref.at[owner_ref[e], pl.ds(0, half)], sems.at[e, 0]
        )
        turned = pltpu.make_async_copy(
            tiles.at[e, pl.ds(half, half)], out_ref.at[other, pl.ds(half, half)], sems.at[e, 1]
        )
        return direct, turned

    def body(e, carry):
        code = table_ref[place_ref[e]]
        lead = (code & 1) == 1
        proj = proj_ref[e]
        marg = margin_ref[e]
        turned = jnp.concatenate([marg[half:], marg[:half]], axis=0)
        left = jnp.where(lead, proj, turned)
        right = jnp.where(lead, marg, proj)
        tiles[e] = (contract_last(left, right) * fock_ref[e]).astype(BF16)
        for copy in copies(e, code >> 1):
            copy.start()
        return carry

    lax.fori_loop(0, edges, body, 0, unroll=8)

    def finish(e, carry):
        for copy in copies(e, 0):
            copy.wait()
        return carry

    lax.fori_loop(0, edges, finish, 0, unroll=8)


def sum_kernel(direct_ref, turned_ref, target_ref, arrived_ref, sent_ref, own_ref, mark_ref, acc, tiles, sems, own_sem):
    half = arrived_ref.shape[1] // 2
    pairs = own_ref.shape[0]
    mark_ref[...] = jnp.zeros_like(mark_ref)
    acc[...] = jnp.zeros_like(acc)

    def body(s, carry):
        acc[direct_ref[s]] += arrived_ref[s, :half, :].astype(F32)
        acc[turned_ref[s]] += arrived_ref[s, half:, :].astype(F32)
        return carry

    lax.fori_loop(0, arrived_ref.shape[0], body, 0, unroll=4)

    def copy(p):
        return pltpu.make_async_copy(tiles.at[p], sent_ref.at[target_ref[p]], sems.at[p])

    def send(p, carry):
        tiles[p] = acc[p].astype(BF16)
        copy(p).start()
        return carry

    lax.fori_loop(0, pairs, send, 0, unroll=4)
    keep = pltpu.make_async_copy(acc.at[pl.ds(0, pairs)], own_ref, own_sem)
    keep.start()

    def finish(p, carry):
        copy(p).wait()
        return carry

    lax.fori_loop(0, pairs, finish, 0, unroll=4)
    keep.wait()


def local_kernel(fock_ref, amps_ref, ints_ref, pno_ref, out_ref):
    rank = amps_ref.shape[1]

    def body(p, carry):
        row = jnp.broadcast_to(pno_ref[p], (rank, rank))
        level = row + row.T - fock_ref[p]
        out_ref[p] = ints_ref[p].astype(F32) + 2.0 * level * amps_ref[p].astype(F32)
        return carry

    lax.fori_loop(0, amps_ref.shape[0], body, 0, unroll=4)


def join_kernel(lead_ref, target_ref, shift_ref, returned_ref, own_ref, local_ref, amps_ref, out_ref, tiles, results, in_sems, out_sems):
    pairs, half, _ = own_ref.shape

    def fetch(p):
        return pltpu.make_async_copy(returned_ref.at[target_ref[p]], tiles.at[p], in_sems.at[p])

    def store(p):
        return pltpu.make_async_copy(results.at[p], out_ref.at[p], out_sems.at[p])

    def start(p, carry):
        fetch(p).start()
        return carry

    def body(p, carry):
        fetch(p).wait()
        own = own_ref[p]
        other = tiles[p].astype(F32)
        rest = local_ref[p] - (2.0 * shift_ref[p]) * amps_ref[p].astype(F32)

        @pl.when(lead_ref[p] == 1)
        def _():
            results[p, :half, :] = (rest[:half] + own).astype(BF16)
            results[p, half:, :] = (rest[half:] + other).astype(BF16)

        @pl.when(lead_ref[p] == 0)
        def _():
            both = jnp.concatenate([other, own], axis=0).T
            results[p] = (rest + both).astype(BF16)

        store(p).start()
        return carry

    def finish(p, carry):
        store(p).wait()
        return carry

    lax.fori_loop(0, pairs, start, 0, unroll=4)
    lax.fori_loop(0, pairs, body, 0, unroll=2)
    lax.fori_loop(0, pairs, finish, 0, unroll=4)


SMEM = pl.BlockSpec(memory_space=pltpu.SMEM)
VMEM = pl.BlockSpec(memory_space=pltpu.VMEM)
HBM = pl.BlockSpec(memory_space=pltpu.HBM)


def call(kernel, name, scalars, arrays, out_shape, out_specs, flops, nbytes, scratch=(), specs=None):
    return pl.pallas_call(
        kernel,
        in_specs=[SMEM] * len(scalars) + (specs or [VMEM] * len(arrays)),
        out_specs=out_specs,
        out_shape=out_shape,
        scratch_shapes=scratch,
        name=name,
        cost_estimate=pl.CostEstimate(flops=flops, bytes_accessed=nbytes, transcendentals=0),
        compiler_params=pltpu.CompilerParams(vmem_limit_bytes=KERNEL_VMEM),
    )(*scalars, *arrays)


def pick_rows(lookup, hit_mask):
    return jnp.sum(jnp.where(hit_mask, lookup[None, :], 0.0), axis=1)


def swapped(value, axis, step):
    members = lax.axis_size(axis)
    return lax.ppermute(value, axis, [(i, i ^ step) for i in range(members)])


def all_sum(value, axis, steps):
    for step in steps:
        value = value + swapped(value, axis, step)
    return value


def powers(stop):
    return [1 << k for k in range(stop.bit_length() - 1)]


def exchange(tiles):
    return lax.all_to_all(tiles, "own", split_axis=0, concat_axis=0, tiled=True)


def local(
    amps, ints, pno_energy, occ_energy, pair_occ, mirror, edge_src, edge_dst, edge_fock, margin
):
    owners = lax.axis_size("own")
    groups = lax.axis_size("grp")
    my_owner = lax.axis_index("own")
    group_index = lax.axis_index("grp")
    pairs, rank, _ = amps.shape
    half = rank // 2
    edges = edge_src.shape[0]
    occ_count = occ_energy.shape[0]
    group_base = group_index * (owners * pairs)
    device_base = group_base + my_owner * pairs
    tile_bytes = rank * rank * 2

    ids = device_base + lax.iota(jnp.int32, pairs)
    lead = ((ids < mirror) ^ ((ids + mirror) % 2 == 1)).astype(jnp.int32)
    mirror_owner = (mirror - group_base) // pairs
    code = jnp.pad(mirror_owner * 2 + lead, (0, LANES - pairs))
    codes = exchange(jnp.broadcast_to(code[None, None, :], (owners, 1, LANES)))
    table = codes.reshape(owners * LANES)

    projected = call(
        project_kernel,
        "project",
        [edge_src - device_base],
        [margin, amps],
        jax.ShapeDtypeStruct((edges, rank, rank), BF16),
        VMEM,
        2 * edges * rank**3,
        (2 * edges + pairs) * tile_bytes,
    )

    group_dst = edge_dst - group_base
    dst_owner = group_dst // pairs
    dst_slot = group_dst % pairs
    my_owner_row = lax.dynamic_slice_in_dim(dst_owner, my_owner * edges, edges)
    my_slot_row = lax.dynamic_slice_in_dim(dst_slot, my_owner * edges, edges)
    outgoing = call(
        couple_kernel,
        "couple",
        [table, my_owner_row * LANES + my_slot_row, my_owner_row, edge_fock],
        [projected, margin],
        pltpu.HBM((owners, rank, rank), BF16),
        HBM,
        2 * edges * rank**3,
        (2 * edges + owners) * tile_bytes,
        [pltpu.VMEM((edges, rank, rank), BF16), pltpu.SemaphoreType.DMA((edges, 2))],
    )
    arrived = exchange(outgoing)

    lane_energy = call(
        energy_kernel,
        "energy",
        [],
        [amps, ints],
        jax.ShapeDtypeStruct((pairs, 1, rank), F32),
        VMEM,
        6 * pairs * rank**2,
        2 * pairs * tile_bytes,
    )
    pair_energy = jnp.sum(lane_energy, axis=(1, 2))
    padded = -(-occ_count // LANES) * LANES
    occ_ids = lax.iota(jnp.int32, padded)
    first_hit = pair_occ[0][:, None] == occ_ids[None, :]
    second_hit = pair_occ[1][:, None] == occ_ids[None, :]
    partial_value = jnp.sum(jnp.where(first_hit, pair_energy[:, None], 0.0), axis=0)
    total = partial_value.reshape(padded // LANES, LANES)
    own_steps = powers(owners)
    total = all_sum(total, "grp", powers(groups))
    total = all_sum(total, "own", own_steps[:-2])
    occ_wide = jnp.pad(occ_energy, (0, padded - occ_count))
    fock_pair = pick_rows(occ_wide, first_hit) + pick_rows(occ_wide, second_hit)

    by_sender = group_dst.reshape(owners, edges)
    direct_hit = by_sender // pairs == my_owner
    direct_row = jnp.max(jnp.where(direct_hit, by_sender % pairs + 1, 0), axis=1)
    mirror_local = mirror - group_base
    turned_hit = by_sender[:, :, None] == mirror_local[None, None, :]
    turned_row = jnp.max(
        jnp.where(turned_hit, lax.iota(jnp.int32, pairs)[None, None, :] + 1, 0), axis=(1, 2)
    )
    direct_row = jnp.where(direct_row == 0, pairs, direct_row - 1)
    turned_row = jnp.where(turned_row == 0, pairs, turned_row - 1)

    total, direct_row = lax.optimization_barrier((total, direct_row))

    sent, own_sum, mark = call(
        sum_kernel,
        "sum",
        [direct_row, turned_row, mirror_owner],
        [arrived],
        [
            pltpu.HBM((owners, half, rank), BF16),
            pltpu.HBM((pairs, half, rank), F32),
            jax.ShapeDtypeStruct((8, LANES), F32),
        ],
        [HBM, HBM, VMEM],
        4 * owners * rank**2,
        (2 * owners + 2 * pairs) * tile_bytes,
        [
            pltpu.VMEM((pairs + 1, half, rank), F32),
            pltpu.VMEM((pairs, half, rank), BF16),
            pltpu.SemaphoreType.DMA((pairs,)),
            pltpu.SemaphoreType.DMA,
        ],
    )
    total, fock_pair, mark = lax.optimization_barrier((total, fock_pair, mark))
    returned = exchange(sent)

    low, high = own_steps[-2:]
    moved = [swapped(total, "own", step) for step in (low, high, low + high)]
    total = total + moved[0] + (moved[1] + moved[2])
    occ_sums = total.reshape(padded)
    shift = 0.5 * (pick_rows(occ_sums, first_hit) + pick_rows(occ_sums, second_hit))
    twice_local = call(
        local_kernel,
        "local",
        [fock_pair],
        [amps, ints, pno_energy.reshape(pairs, 1, rank)],
        jax.ShapeDtypeStruct((pairs, rank, rank), F32),
        VMEM,
        6 * pairs * rank**2,
        4 * pairs * tile_bytes,
    )
    return call(
        join_kernel,
        "join",
        [lead, mirror_owner, shift],
        [returned, own_sum, twice_local, amps],
        pltpu.HBM((pairs, rank, rank), BF16),
        HBM,
        pairs * rank**2,
        (owners // 2 + 2 * pairs) * tile_bytes,
        [
            pltpu.VMEM((pairs, half, rank), BF16),
            pltpu.VMEM((pairs, rank, rank), BF16),
            pltpu.SemaphoreType.DMA((pairs,)),
            pltpu.SemaphoreType.DMA((pairs,)),
        ],
        [HBM, VMEM, VMEM, VMEM],
    )


def solution(mesh):
    in_specs = (
        P(("grp", "own"), None, None),
        P(("grp", "own"), None, None),
        P(("grp", "own"), None),
        P(),
        P(None, ("grp", "own")),
        P(("grp", "own")),
        P(("grp", "own")),
        P("grp"),
        P(("grp", "own")),
        P(("grp", "own"), None, None),
    )
    out_specs = P(("grp", "own"), None, None)
    return jax.shard_map(local, mesh=mesh, in_specs=in_specs, out_specs=out_specs, check_vma=False)
```

time: 257 us -> 131 us (0.51)
  blocking collectives: 137 us -> 0 us
  starting transfers between devices: 20.4 us -> 73.7 us
  local copies, waits for them, and re-layouts: 29.9 us -> 6.94 us
  waiting for transfers between devices: 49.6 us -> 28.9 us
  Pallas kernels: 0 us -> 16.1 us
  matrix products: 8.65 us -> 0 us
  other arithmetic: 9.49 us -> 3.37 us
    psum x1 -> x0, blocking collectives: 137 us -> none  [local(): occ_sums = lax.psum(partial_value, ('grp', 'own'))]
    ppermute x0 -> x10, starting transfers between devices: none -> 45.9 us  [swapped(): return lax.ppermute(value, axis, [(i, i ^ step) for i in range(members)])]
    all_to_all x2 -> x3, waiting for transfers between devices: 49.6 us -> 6.84 us  [exchange(): return lax.all_to_all(tiles, 'own', split_axis=0, concat_axis=0, tiled=True)]
    ppermute x0 -> x10, waiting for transfers between devices: none -> 22 us  [swapped(): return lax.ppermute(value, axis, [(i, i ^ step) for i in range(members)])]
    pallas_call x0 -> x6, Pallas kernels: none -> 16.1 us  [call(): pl.pallas_call(kernel, in_specs=[SMEM] * len(scalars) + (specs or [VMEM]...]
    scatter x2 -> x0, local copies, waits for them, and re-layouts: 11.1 us -> none  [the longest x1 6.59 us: pack_tiles(): return blank_buffer.at[placed].set(tile_set)]
    dot_general x2 -> x0, matrix products: 8.65 us -> none  [the longest x1 4.92 us: arrival_sum(): jnp.dot(selector, arrived.reshape(owners * capacity, tile_rows * tile_col...]
    all_to_all x2 -> x3, starting transfers between devices: 20.4 us -> 27.8 us  [exchange(): return lax.all_to_all(tiles, 'own', split_axis=0, concat_axis=0, tiled=True)]
  transfers between devices with their start and end apart: 2 -> 13, of which waited for: 1 -> 12; matrix products, arithmetic and copies ran while one was open for 2% -> 2% of each run, Pallas kernels for 0% -> 3%
where the time goes in v2:
time: 131 us; the launch traced here: 129 us
  starting transfers between devices  73.7 us (56%)
  waiting for transfers between devices  28.9 us (22%)
  Pallas kernels  16.1 us (12%)
  local copies, waits for them, and re-layouts  6.94 us (5%)
  other arithmetic  3.37 us (3%)
    ppermute x10, starting transfers between devices, swapped(): return lax.ppermute(value, axis, [(i, i ^ step) for i in range(members)])  45.9 us
    all_to_all x3, starting transfers between devices, exchange(): return lax.all_to_all(tiles, 'own', split_axis=0, concat_axis=0, tiled=True)  27.8 us
    ppermute x10, waiting for transfers between devices, swapped(): return lax.ppermute(value, axis, [(i, i ^ step) for i in range(members)])  22 us
    pallas_call x6, Pallas kernels, call(): pl.pallas_call(kernel, in_specs=[SMEM] * len(scalars) + (specs or [VMEM]...  16.1 us
    all_to_all x3, waiting for transfers between devices, exchange(): return lax.all_to_all(tiles, 'own', split_axis=0, concat_axis=0, tiled=True)  6.84 us
    unnamed x22, local copies, waits for them, and re-layouts  6.14 us
  transfers between devices with their start and end apart: 13, of which 12 were waited for; matrix products, arithmetic and copies ran while one was open for 2% of the time, Pallas kernels for 3%

profile of v2, /device:TPU:1, one launch (start us, length us, event | category | flops | bytes accessed | tf_op | source)
XLA Modules:
  0.0 129.3 jit_solution(9582590592651434046)
XLA Ops:
  1.3 11.6 %all-to-all-start = ((s32[64,1,128]{2,1,0:T(1,128)}), s32[64,1,128]{2,1,0:T(1,128)S(1)}, u32[]{:S(2)}, u32[]{:S(2)}) async-start(s32[64,1,128]{2,1,0:T(1,128)} %broadcast_in_dim.78), calls=%async_computation | async-start | bytes 65536 | tf_op jit(solution)/shard_map/all_to_all | solution.py:197
  14.4 1.2 copy-done
  15.6 1.4 %copy-done.2 = bf16[48,128,128]{2,1,0:T(8,128)(2,1)S(1)} copy-done((bf16[48,128,128]{2,1,0:T(8,128)(2,1)S(1)}, bf16[48,128,128]{2,1,0:T(8,128)(2,1)}, u32[]{:S(2)}) %copy-start.2) | copy-done | bytes 1572888
  17.0 1.9 %project.1.proj_ref = bf16[48,128,128]{2,1,0:T(8,128)(2,1)S(1)} custom-call(s32[48]{0:T(128)S(1)} %broadcast_subtract_fusion.1.src_ref, bf16[48,128,128]{2,1,0:T(8,128)(2,1)S(1)} %copy-done.2, bf16[28,128,128]{2,1,0:T(8,128)(2,1)S(1)} %copy-done), custom_call_target="tpu_custom_call" | custom-call | flops 201326592 | bytes 4063232 | tf_op jit(solution)/shard_map/project/pallas_call | solution.py:165
  18.9 3.3 %all-to-all-done = s32[64,1,128]{2,1,0:T(1,128)S(1)} async-done(((s32[64,1,128]{2,1,0:T(1,128)}), s32[64,1,128]{2,1,0:T(1,128)S(1)}, u32[]{:S(2)}, u32[]{:S(2)}) %all-to-all-start) | async-done | bytes 32800 | tf_op jit(solution)/shard_map/all_to_all | solution.py:197
  22.3 4.5 %couple.1 = bf16[64,128,128]{2,1,0:T(8,128)(2,1)} custom-call(s32[8192]{0:T(1024)S(1)} %bitcast.11, s32[48]{0:T(128)S(1)} %get-tuple-element.22.place_ref, s32[48]{0:T(128)S(1)} %get-tuple-element.23.owner_ref, f32[48]{0:T(128)S(1)} %copy-done.7, bf16[48,128,128]{2,1,0:T(8,128)(2,1)S(1)} %project.1.proj_ref, bf16[48,128,128]{2,1,0:T(8,128)(2,1)S(1)} %copy-done.3), custom_call_target="tpu_custom_call" | custom-call | flops 201326592 | bytes 5242880 | tf_op jit(solution)/shard_map/couple/pallas_call | solution.py:165
  26.8 7.2 %all-to-all-start.1 = ((bf16[64,128,128]{2,1,0:T(8,128)(2,1)}), bf16[64,128,128]{2,1,0:T(8,128)(2,1)S(1)}, u32[]{:S(2)}, u32[]{:S(2)}) async-start(bf16[64,128,128]{2,1,0:T(8,128)(2,1)} %couple.1), calls=%async_computation.1 | async-start | bytes 4194304 | tf_op jit(solution)/shard_map/all_to_all | solution.py:197
  34.0 1.2 copy-done.4
  36.6 4.0 %collective-permute-start = (f32[8,128]{1,0:T(8,128)S(1)}, f32[8,128]{1,0:T(8,128)S(1)}, u32[]{:S(2)}, u32[]{:S(2)}) collective-permute-start(f32[8,128]{1,0:T(8,128)S(1)} %bitcast.12), channel_id=1, source_target_pairs={{0,64},{64,0},{128,192},{192,128},{256,320},{320,256},{384,448},{4... | collective-permute-start | bytes 12296 | tf_op jit(solution)/shard_map/ppermute | solution.py:183
  40.6 1.3 collective-permute-done
  41.9 5.8 %collective-permute-start.1 = (f32[8,128]{1,0:T(8,128)S(1)}, f32[8,128]{1,0:T(8,128)S(1)}, u32[]{:S(2)}, u32[]{:S(2)}) collective-permute-start(f32[8,128]{1,0:T(8,128)S(1)} %bitcast_add_fusion), channel_id=1, source_target_pairs={{0,128},{64,192},{128,0},{192,64},{256,384},{320,448},{384,256},{4... | collective-permute-start | bytes 12296 | tf_op jit(solution)/shard_map/ppermute | solution.py:183
  48.6 8.7 %collective-permute-start.2 = (f32[8,128]{1,0:T(8,128)S(1)}, f32[8,128]{1,0:T(8,128)S(1)}, u32[]{:S(2)}, u32[]{:S(2)}) collective-permute-start(f32[8,128]{1,0:T(8,128)S(1)} %fusion.7), channel_id=1, source_target_pairs={{0,256},{64,320},{128,384},{192,448},{256,0},{320,64},{384,128},{4... | collective-permute-start | bytes 12296 | tf_op jit(solution)/shard_map/ppermute | solution.py:183
  57.5 1.1 collective-permute-done.2
  58.7 4.6 %collective-permute-start.3 = (f32[8,128]{1,0:T(8,128)S(1)}, f32[8,128]{1,0:T(8,128)S(1)}, u32[]{:S(2)}, u32[]{:S(2)}) collective-permute-start(f32[8,128]{1,0:T(8,128)S(1)} %add.104), channel_id=1, source_target_pairs={{0,1},{1,0},{2,3},{3,2},{4,5},{5,4},{6,7},{7,6},{8,9},{9,8},{10,11... | collective-permute-start | bytes 12296 | tf_op jit(solution)/shard_map/ppermute | solution.py:183
  64.1 3.2 %collective-permute-start.4 = (f32[8,128]{1,0:T(8,128)S(1)}, f32[8,128]{1,0:T(8,128)S(1)}, u32[]{:S(2)}, u32[]{:S(2)}) collective-permute-start(f32[8,128]{1,0:T(8,128)S(1)} %add.105), channel_id=1, source_target_pairs={{0,2},{1,3},{2,0},{3,1},{4,6},{5,7},{6,4},{7,5},{8,10},{9,11},{10,... | collective-permute-start | bytes 12296 | tf_op jit(solution)/shard_map/ppermute | solution.py:183
  67.3 1.4 %collective-permute-done.4 = f32[8,128]{1,0:T(8,128)S(1)} collective-permute-done((f32[8,128]{1,0:T(8,128)S(1)}, f32[8,128]{1,0:T(8,128)S(1)}, u32[]{:S(2)}, u32[]{:S(2)}) %collective-permute-start.4) | collective-permute-done | bytes 4128 | tf_op jit(solution)/shard_map/ppermute | solution.py:183
  68.8 4.7 %collective-permute-start.5 = (f32[8,128]{1,0:T(8,128)S(1)}, f32[8,128]{1,0:T(8,128)S(1)}, u32[]{:S(2)}, u32[]{:S(2)}) collective-permute-start(f32[8,128]{1,0:T(8,128)S(1)} %add.106), channel_id=1, source_target_pairs={{0,4},{1,5},{2,6},{3,7},{4,0},{5,1},{6,2},{7,3},{8,12},{9,13},{10,... | collective-permute-start | bytes 12296 | tf_op jit(solution)/shard_map/ppermute | solution.py:183
  73.6 1.4 %collective-permute-done.5 = f32[8,128]{1,0:T(8,128)S(1)} collective-permute-done((f32[8,128]{1,0:T(8,128)S(1)}, f32[8,128]{1,0:T(8,128)S(1)}, u32[]{:S(2)}, u32[]{:S(2)}) %collective-permute-start.5) | collective-permute-done | bytes 4128 | tf_op jit(solution)/shard_map/ppermute | solution.py:183
  75.0 3.3 %collective-permute-start.6 = (f32[8,128]{1,0:T(8,128)S(1)}, f32[8,128]{1,0:T(8,128)S(1)}, u32[]{:S(2)}, u32[]{:S(2)}) collective-permute-start(f32[8,128]{1,0:T(8,128)S(1)} %add.107), channel_id=1, source_target_pairs={{0,8},{1,9},{2,10},{3,11},{4,12},{5,13},{6,14},{7,15},{8,0},{9,1},... | collective-permute-start | bytes 12296 | tf_op jit(solution)/shard_map/ppermute | solution.py:183
  78.3 2.3 %collective-permute-done.6 = f32[8,128]{1,0:T(8,128)S(1)} collective-permute-done((f32[8,128]{1,0:T(8,128)S(1)}, f32[8,128]{1,0:T(8,128)S(1)}, u32[]{:S(2)}, u32[]{:S(2)}) %collective-permute-start.6) | collective-permute-done | bytes 4128 | tf_op jit(solution)/shard_map/ppermute | solution.py:183
  80.7 3.0 %all-to-all-done.1.arrived_ref = bf16[64,128,128]{2,1,0:T(8,128)(2,1)S(1)} async-done(((bf16[64,128,128]{2,1,0:T(8,128)(2,1)}), bf16[64,128,128]{2,1,0:T(8,128)(2,1)S(1)}, u32[]{:S(2)}, u32[]{:S(2)}) %all-to-all-start.1) | async-done | bytes 2097184 | tf_op jit(solution)/shard_map/all_to_all | solution.py:197
  83.7 3.2 %sum.1 = (bf16[64,64,128]{2,1,0:T(8,128)(2,1)}, f32[28,64,128]{2,1,0:T(8,128)}, f32[8,128]{1,0:T(8,128)}) custom-call(s32[64]{0:T(128)S(1)} %compare_select_fusion.3.direct_ref, s32[64]{0:T(128)S(1)} %compare_select_fusion.2.turned_ref, s32[28]{0:T(128)S(1)} %get-tuple-element.27.target_ref, bf16[64,128,128]{2,1,0:T(8,128)(2,1)S(1)} %all-to-all-done.1.arrived_ref), custom_call_target="tpu_custom_call" | custom-call | flops 4194304 | bytes 6029312 | tf_op jit(solution)/shard_map/sum/pallas_call | solution.py:165
  86.9 9.1 %all-to-all-start.2 = ((bf16[64,64,128]{2,1,0:T(8,128)(2,1)}), bf16[64,64,128]{2,1,0:T(8,128)(2,1)}, u32[]{:S(2)}, u32[]{:S(2)}) async-start(bf16[64,64,128]{2,1,0:T(8,128)(2,1)} %get-tuple-element.14), calls=%async_computation.2 | async-start | bytes 2097152 | tf_op jit(solution)/shard_map/all_to_all | solution.py:197
  96.0 5.6 %collective-permute-start.9 = (f32[8,128]{1,0:T(8,128)S(1)}, f32[8,128]{1,0:T(8,128)S(1)}, u32[]{:S(2)}, u32[]{:S(2)}) collective-permute-start(f32[8,128]{1,0:T(8,128)S(1)} %add.108), channel_id=1, source_target_pairs={{0,48},{1,49},{2,50},{3,51},{4,52},{5,53},{6,54},{7,55},{8,56},{9,... | collective-permute-start | bytes 12296 | tf_op jit(solution)/shard_map/ppermute | solution.py:183
  101.6 3.8 %collective-permute-start.8 = (f32[8,128]{1,0:T(8,128)S(1)}, f32[8,128]{1,0:T(8,128)S(1)}, u32[]{:S(2)}, u32[]{:S(2)}) collective-permute-start(f32[8,128]{1,0:T(8,128)S(1)} %add.108), channel_id=1, source_target_pairs={{0,32},{1,33},{2,34},{3,35},{4,36},{5,37},{6,38},{7,39},{8,40},{9,... | collective-permute-start | bytes 12296 | tf_op jit(solution)/shard_map/ppermute | solution.py:183
  105.4 2.1 %collective-permute-start.7 = (f32[8,128]{1,0:T(8,128)S(1)}, f32[8,128]{1,0:T(8,128)S(1)}, u32[]{:S(2)}, u32[]{:S(2)}) collective-permute-start(f32[8,128]{1,0:T(8,128)S(1)} %add.108), channel_id=1, source_target_pairs={{0,16},{1,17},{2,18},{3,19},{4,20},{5,21},{6,22},{7,23},{8,24},{9,... | collective-permute-start | bytes 12296 | tf_op jit(solution)/shard_map/ppermute | solution.py:183
  107.6 1.2 copy-done.5
  108.7 1.5 %local.1.local_ref = f32[28,128,128]{2,1,0:T(8,128)S(1)} custom-call(f32[28]{0:T(128)S(1)} %add.111.fock_ref, bf16[28,128,128]{2,1,0:T(8,128)(2,1)S(1)} %copy-done.1, bf16[28,128,128]{2,1,0:T(8,128)(2,1)S(1)} %copy-done.5, f32[28,1,128]{2,1,0:T(1,128)S(1)} %reshape.30.pno_ref), custom_call_target="tpu_custom_call" | custom-call | flops 2752512 | bytes 3670016 | tf_op jit(solution)/shard_map/local/pallas_call | solution.py:165
  110.2 11.5 %collective-permute-done.9 = f32[8,128]{1,0:T(8,128)S(1)} collective-permute-done((f32[8,128]{1,0:T(8,128)S(1)}, f32[8,128]{1,0:T(8,128)S(1)}, u32[]{:S(2)}, u32[]{:S(2)}) %collective-permute-start.9) | collective-permute-done | bytes 4128 | tf_op jit(solution)/shard_map/ppermute | solution.py:183
  121.8 1.5 %collective-permute-done.8 = f32[8,128]{1,0:T(8,128)S(1)} collective-permute-done((f32[8,128]{1,0:T(8,128)S(1)}, f32[8,128]{1,0:T(8,128)S(1)}, u32[]{:S(2)}, u32[]{:S(2)}) %collective-permute-start.8) | collective-permute-done | bytes 4128 | tf_op jit(solution)/shard_map/ppermute | solution.py:183
  124.0 1.2 copy-done.6
  125.2 4.1 %join.1 = bf16[28,128,128]{2,1,0:T(8,128)(2,1)} custom-call(s32[28]{0:T(128)S(1)} %get-tuple-element.29.lead_ref, s32[28]{0:T(128)S(1)} %get-tuple-element.27.target_ref, f32[28]{0:T(128)S(1)} %add_multiply_fusion.shift_ref, bf16[64,64,128]{2,1,0:T(8,128)(2,1)} %all-to-all-done.2.returned_ref, f32[28,64,128]{2,1,0:T(8,128)S(1)} %copy-done.6, ...), custom_call_target="tpu_custom_call" | custom-call | flops 458752 | bytes 2883584 | tf_op jit(solution)/shard_map/join/pallas_call | solution.py:165
  (51 shorter events, 7.1 us)
Async XLA Ops:
  1.3 20.9 %all-to-all-start = ((s32[64,1,128]{2,1,0:T(1,128)}), s32[64,1,128]{2,1,0:T(1,128)S(1)}, u32[]{:S(2)}, u32[]{:S(2)}) async-start(s32[64,1,128]{2,1,0:T(1,128)} %broadcast_in_dim.78), calls=%async_computation | async-start | bytes 65536 | tf_op jit(solution)/shard_map/all_to_all | solution.py:197
  14.4 1.2 copy-start
  15.6 1.4 %copy-start.2 = (bf16[48,128,128]{2,1,0:T(8,128)(2,1)S(1)}, bf16[48,128,128]{2,1,0:T(8,128)(2,1)}, u32[]{:S(2)}) copy-start(bf16[48,128,128]{2,1,0:T(8,128)(2,1)} %margin_ref.3) | copy-start | bytes 4718596
  17.0 5.2 %copy-start.3 = (bf16[48,128,128]{2,1,0:T(8,128)(2,1)S(1)}, bf16[48,128,128]{2,1,0:T(8,128)(2,1)}, u32[]{:S(2)}) copy-start(bf16[48,128,128]{2,1,0:T(8,128)(2,1)} %margin_ref.3) | copy-start | bytes 4718596
  17.0 5.2 %copy-start.7 = (f32[48]{0:T(128)S(1)}, f32[48]{0:T(128)}, u32[]{:S(2)}) copy-start(f32[48]{0:T(128)} %fock_ref.1) | copy-start | bytes 580
  26.8 7.2 %copy-start.9 = (f32[1000]{0:T(1024)S(1)}, f32[1000]{0:T(1024)}, u32[]{:S(2)}) copy-start(f32[1000]{0:T(1024)} %param.13) | copy-start | bytes 12004
  26.8 7.2 %copy-start.1 = (bf16[28,128,128]{2,1,0:T(8,128)(2,1)S(1)}, bf16[28,128,128]{2,1,0:T(8,128)(2,1)}, u32[]{:S(2)}) copy-start(bf16[28,128,128]{2,1,0:T(8,128)(2,1)} %amps_ref.7) | copy-start | bytes 2752516
  26.8 56.9 %all-to-all-start.1 = ((bf16[64,128,128]{2,1,0:T(8,128)(2,1)}), bf16[64,128,128]{2,1,0:T(8,128)(2,1)S(1)}, u32[]{:S(2)}, u32[]{:S(2)}) async-start(bf16[64,128,128]{2,1,0:T(8,128)(2,1)} %couple.1), calls=%async_computation.1 | async-start | bytes 4194304 | tf_op jit(solution)/shard_map/all_to_all | solution.py:197
  34.0 2.4 %copy-start.10 = (s32[2,28]{1,0:T(2,128)S(1)}, s32[2,28]{1,0:T(2,128)}, u32[]{:S(2)}) copy-start(s32[2,28]{1,0:T(2,128)} %param.14) | copy-start | bytes 676
  34.0 1.2 copy-start.4
  36.6 5.3 %collective-permute-start = (f32[8,128]{1,0:T(8,128)S(1)}, f32[8,128]{1,0:T(8,128)S(1)}, u32[]{:S(2)}, u32[]{:S(2)}) collective-permute-start(f32[8,128]{1,0:T(8,128)S(1)} %bitcast.12), channel_id=1, source_target_pairs={{0,64},{64,0},{128,192},{192,128},{256,320},{320,256},{384,448},{4... | collective-permute-start | bytes 12296 | tf_op jit(solution)/shard_map/ppermute | solution.py:183
  41.9 6.8 %collective-permute-start.1 = (f32[8,128]{1,0:T(8,128)S(1)}, f32[8,128]{1,0:T(8,128)S(1)}, u32[]{:S(2)}, u32[]{:S(2)}) collective-permute-start(f32[8,128]{1,0:T(8,128)S(1)} %bitcast_add_fusion), channel_id=1, source_target_pairs={{0,128},{64,192},{128,0},{192,64},{256,384},{320,448},{384,256},{4... | collective-permute-start | bytes 12296 | tf_op jit(solution)/shard_map/ppermute | solution.py:183
  48.6 10.0 %collective-permute-start.2 = (f32[8,128]{1,0:T(8,128)S(1)}, f32[8,128]{1,0:T(8,128)S(1)}, u32[]{:S(2)}, u32[]{:S(2)}) collective-permute-start(f32[8,128]{1,0:T(8,128)S(1)} %fusion.7), channel_id=1, source_target_pairs={{0,256},{64,320},{128,384},{192,448},{256,0},{320,64},{384,128},{4... | collective-permute-start | bytes 12296 | tf_op jit(solution)/shard_map/ppermute | solution.py:183
  58.7 5.4 %collective-permute-start.3 = (f32[8,128]{1,0:T(8,128)S(1)}, f32[8,128]{1,0:T(8,128)S(1)}, u32[]{:S(2)}, u32[]{:S(2)}) collective-permute-start(f32[8,128]{1,0:T(8,128)S(1)} %add.104), channel_id=1, source_target_pairs={{0,1},{1,0},{2,3},{3,2},{4,5},{5,4},{6,7},{7,6},{8,9},{9,8},{10,11... | collective-permute-start | bytes 12296 | tf_op jit(solution)/shard_map/ppermute | solution.py:183
  64.1 4.6 %collective-permute-start.4 = (f32[8,128]{1,0:T(8,128)S(1)}, f32[8,128]{1,0:T(8,128)S(1)}, u32[]{:S(2)}, u32[]{:S(2)}) collective-permute-start(f32[8,128]{1,0:T(8,128)S(1)} %add.105), channel_id=1, source_target_pairs={{0,2},{1,3},{2,0},{3,1},{4,6},{5,7},{6,4},{7,5},{8,10},{9,11},{10,... | collective-permute-start | bytes 12296 | tf_op jit(solution)/shard_map/ppermute | solution.py:183
  68.8 6.2 %collective-permute-start.5 = (f32[8,128]{1,0:T(8,128)S(1)}, f32[8,128]{1,0:T(8,128)S(1)}, u32[]{:S(2)}, u32[]{:S(2)}) collective-permute-start(f32[8,128]{1,0:T(8,128)S(1)} %add.106), channel_id=1, source_target_pairs={{0,4},{1,5},{2,6},{3,7},{4,0},{5,1},{6,2},{7,3},{8,12},{9,13},{10,... | collective-permute-start | bytes 12296 | tf_op jit(solution)/shard_map/ppermute | solution.py:183
  75.0 5.7 %collective-permute-start.6 = (f32[8,128]{1,0:T(8,128)S(1)}, f32[8,128]{1,0:T(8,128)S(1)}, u32[]{:S(2)}, u32[]{:S(2)}) collective-permute-start(f32[8,128]{1,0:T(8,128)S(1)} %add.107), channel_id=1, source_target_pairs={{0,8},{1,9},{2,10},{3,11},{4,12},{5,13},{6,14},{7,15},{8,0},{9,1},... | collective-permute-start | bytes 12296 | tf_op jit(solution)/shard_map/ppermute | solution.py:183
  83.7 23.8 %copy-start.8 = (f32[28,128]{1,0:T(8,128)S(1)}, f32[28,128]{1,0:T(8,128)}, u32[]{:S(2)}) copy-start(f32[28,128]{1,0:T(8,128)} %param.12) | copy-start | bytes 43012
  86.9 37.1 %all-to-all-start.2 = ((bf16[64,64,128]{2,1,0:T(8,128)(2,1)}), bf16[64,64,128]{2,1,0:T(8,128)(2,1)}, u32[]{:S(2)}, u32[]{:S(2)}) async-start(bf16[64,64,128]{2,1,0:T(8,128)(2,1)} %get-tuple-element.14), calls=%async_computation.2 | async-start | bytes 2097152 | tf_op jit(solution)/shard_map/all_to_all | solution.py:197
  96.0 25.8 %collective-permute-start.9 = (f32[8,128]{1,0:T(8,128)S(1)}, f32[8,128]{1,0:T(8,128)S(1)}, u32[]{:S(2)}, u32[]{:S(2)}) collective-permute-start(f32[8,128]{1,0:T(8,128)S(1)} %add.108), channel_id=1, source_target_pairs={{0,48},{1,49},{2,50},{3,51},{4,52},{5,53},{6,54},{7,55},{8,56},{9,... | collective-permute-start | bytes 12296 | tf_op jit(solution)/shard_map/ppermute | solution.py:183
  101.6 21.6 %collective-permute-start.8 = (f32[8,128]{1,0:T(8,128)S(1)}, f32[8,128]{1,0:T(8,128)S(1)}, u32[]{:S(2)}, u32[]{:S(2)}) collective-permute-start(f32[8,128]{1,0:T(8,128)S(1)} %add.108), channel_id=1, source_target_pairs={{0,32},{1,33},{2,34},{3,35},{4,36},{5,37},{6,38},{7,39},{8,40},{9,... | collective-permute-start | bytes 12296 | tf_op jit(solution)/shard_map/ppermute | solution.py:183
  105.4 17.9 %collective-permute-start.7 = (f32[8,128]{1,0:T(8,128)S(1)}, f32[8,128]{1,0:T(8,128)S(1)}, u32[]{:S(2)}, u32[]{:S(2)}) collective-permute-start(f32[8,128]{1,0:T(8,128)S(1)} %add.108), channel_id=1, source_target_pairs={{0,16},{1,17},{2,18},{3,19},{4,20},{5,21},{6,22},{7,23},{8,24},{9,... | collective-permute-start | bytes 12296 | tf_op jit(solution)/shard_map/ppermute | solution.py:183
  107.5 1.2 copy-start.5
  124.0 1.2 copy-start.6

commit v3 on v2

--- a/solution.py
+++ b/solution.py
@@ -1,3 +1,5 @@
+import functools
+
 import jax
 import jax.numpy as jnp
 from jax import lax
@@ -34,9 +36,16 @@
     lax.fori_loop(0, amps_ref.shape[0], body, 0, unroll=4)
 
 
-def couple_kernel(table_ref, place_ref, owner_ref, fock_ref, proj_ref, margin_ref, out_ref, tiles, sems):
-    half = margin_ref.shape[1] // 2
-    edges = margin_ref.shape[0]
+def leads(pair, other):
+    return ((pair < other) ^ ((pair + other) % 2 == 1)).astype(jnp.int32)
+
+
+def couple_kernel(pairs, base_ref, table_ref, place_ref, owner_ref, pair_ref, fock_ref, proj_ref, margin_ref, out_ref, tiles, sems):
+    edges = tiles.shape[0]
+    half = tiles.shape[1] // 2
+    scale = -(-(1 << 20) // pairs)
+    reach = pairs * out_ref.shape[0]
+    assert all(x * scale >> 20 == x // pairs for x in range(reach)) and reach * scale < 2**31
 
     def copies(e, other):
         direct = pltpu.make_async_copy(
@@ -47,113 +56,128 @@
         )
         return direct, turned
 
-    def body(e, carry):
-        code = table_ref[place_ref[e]]
-        lead = (code & 1) == 1
+    def start(e, carry):
+        twin = table_ref[place_ref[e]]
+        pair = pair_ref[e]
+        lead = (((pair < twin).astype(jnp.int32) + pair + twin) & 1) == 1
+        other = ((twin - base_ref[0]) * scale) >> 20
         proj = proj_ref[e]
         marg = margin_ref[e]
         turned = jnp.concatenate([marg[half:], marg[:half]], axis=0)
         left = jnp.where(lead, proj, turned)
         right = jnp.where(lead, marg, proj)
         tiles[e] = (contract_last(left, right) * fock_ref[e]).astype(BF16)
-        for copy in copies(e, code >> 1):
+        for copy in copies(e, other):
             copy.start()
         return carry
-
-    lax.fori_loop(0, edges, body, 0, unroll=8)
 
     def finish(e, carry):
         for copy in copies(e, 0):
             copy.wait()
         return carry
 
+    lax.fori_loop(0, edges, start, 0, unroll=8)
     lax.fori_loop(0, edges, finish, 0, unroll=8)
 
 
-def sum_kernel(direct_ref, turned_ref, target_ref, arrived_ref, sent_ref, own_ref, mark_ref, acc, tiles, sems, own_sem):
+def sum_kernel(direct_ref, turned_ref, target_ref, arrived_ref, sent_ref, mark_ref, direct_acc, turned_acc, tiles, sems):
     half = arrived_ref.shape[1] // 2
-    pairs = own_ref.shape[0]
+    pairs = tiles.shape[0]
     mark_ref[...] = jnp.zeros_like(mark_ref)
-    acc[...] = jnp.zeros_like(acc)
+    direct_acc[...] = jnp.zeros_like(direct_acc)
+    turned_acc[...] = jnp.zeros_like(turned_acc)
 
     def body(s, carry):
-        acc[direct_ref[s]] += arrived_ref[s, :half, :].astype(F32)
-        acc[turned_ref[s]] += arrived_ref[s, half:, :].astype(F32)
-        return carry
-
-    lax.fori_loop(0, arrived_ref.shape[0], body, 0, unroll=4)
+        direct_acc[direct_ref[s]] += arrived_ref[s, :half, :].astype(F32)
+        turned_acc[turned_ref[s]] += arrived_ref[s, half:, :].astype(F32)
+        return carry
+
+    lax.fori_loop(0, arrived_ref.shape[0], body, 0, unroll=8)
 
     def copy(p):
         return pltpu.make_async_copy(tiles.at[p], sent_ref.at[target_ref[p]], sems.at[p])
 
     def send(p, carry):
-        tiles[p] = acc[p].astype(BF16)
+        tiles[p] = (direct_acc[p] + turned_acc[p]).astype(BF16)
         copy(p).start()
         return carry
-
-    lax.fori_loop(0, pairs, send, 0, unroll=4)
-    keep = pltpu.make_async_copy(acc.at[pl.ds(0, pairs)], own_ref, own_sem)
-    keep.start()
 
     def finish(p, carry):
         copy(p).wait()
         return carry
 
+    lax.fori_loop(0, pairs, send, 0, unroll=4)
     lax.fori_loop(0, pairs, finish, 0, unroll=4)
-    keep.wait()
-
-
-def local_kernel(fock_ref, amps_ref, ints_ref, pno_ref, out_ref):
+
+
+def unit(rank):
+    rows = lax.broadcasted_iota(jnp.int32, (rank, rank), 0)
+    columns = lax.broadcasted_iota(jnp.int32, (rank, rank), 1)
+    return (rows == columns).astype(F32).astype(BF16)
+
+
+def local_kernel(lead_ref, target_ref, fock_ref, amps_ref, ints_ref, pno_ref, sent_ref, out_ref, mark_ref, results, sem):
     rank = amps_ref.shape[1]
+    one = unit(rank)
+    mark_ref[...] = jnp.zeros_like(mark_ref)
 
     def body(p, carry):
         row = jnp.broadcast_to(pno_ref[p], (rank, rank))
         level = row + row.T - fock_ref[p]
-        out_ref[p] = ints_ref[p].astype(F32) + 2.0 * level * amps_ref[p].astype(F32)
+        twice = ints_ref[p].astype(F32) + 2.0 * level * amps_ref[p].astype(F32)
+        own = sent_ref[target_ref[p]]
+        none = jnp.zeros_like(own)
+        upper = jnp.concatenate([own, none], axis=0).astype(F32)
+        right = contract_last(one, jnp.concatenate([none, own], axis=0))
+        results[p] = twice + jnp.where(lead_ref[p] == 1, upper, right)
         return carry
 
     lax.fori_loop(0, amps_ref.shape[0], body, 0, unroll=4)
-
-
-def join_kernel(lead_ref, target_ref, shift_ref, returned_ref, own_ref, local_ref, amps_ref, out_ref, tiles, results, in_sems, out_sems):
-    pairs, half, _ = own_ref.shape
+    copy = pltpu.make_async_copy(results, out_ref, sem)
+    copy.start()
+    copy.wait()
+
+
+def join_kernel(lead_ref, target_ref, shift_ref, returned_ref, local_ref, amps_ref, out_ref, tiles, locals_, results, sems, in_sems, out_sems):
+    pairs, half, rank = tiles.shape
+    chunks = in_sems.shape[0]
+    count = pairs // chunks
+    one = unit(rank)
 
     def fetch(p):
-        return pltpu.make_async_copy(returned_ref.at[target_ref[p]], tiles.at[p], in_sems.at[p])
-
-    def store(p):
-        return pltpu.make_async_copy(results.at[p], out_ref.at[p], out_sems.at[p])
-
-    def start(p, carry):
-        fetch(p).start()
-        return carry
-
-    def body(p, carry):
-        fetch(p).wait()
-        own = own_ref[p]
-        other = tiles[p].astype(F32)
-        rest = local_ref[p] - (2.0 * shift_ref[p]) * amps_ref[p].astype(F32)
-
-        @pl.when(lead_ref[p] == 1)
-        def _():
-            results[p, :half, :] = (rest[:half] + own).astype(BF16)
-            results[p, half:, :] = (rest[half:] + other).astype(BF16)
-
-        @pl.when(lead_ref[p] == 0)
-        def _():
-            both = jnp.concatenate([other, own], axis=0).T
-            results[p] = (rest + both).astype(BF16)
-
-        store(p).start()
-        return carry
-
-    def finish(p, carry):
-        store(p).wait()
-        return carry
-
-    lax.fori_loop(0, pairs, start, 0, unroll=4)
-    lax.fori_loop(0, pairs, body, 0, unroll=2)
-    lax.fori_loop(0, pairs, finish, 0, unroll=4)
+        return pltpu.make_async_copy(returned_ref.at[target_ref[p]], tiles.at[p], sems.at[p])
+
+    def load(k):
+        rows = pl.ds(k * count, count)
+        return pltpu.make_async_copy(local_ref.at[rows], locals_.at[rows], in_sems.at[k])
+
+    def store(k):
+        rows = pl.ds(k * count, count)
+        return pltpu.make_async_copy(results.at[rows], out_ref.at[rows], out_sems.at[k])
+
+    for k in range(chunks):
+        load(k).start()
+        for p in range(k * count, (k + 1) * count):
+            fetch(p).start()
+
+    def body(k, carry):
+        load(k).wait()
+        for i in range(count):
+            fetch(k * count + i).wait()
+        for i in range(count):
+            p = k * count + i
+            other = tiles[p]
+            none = jnp.zeros_like(other)
+            lower = jnp.concatenate([none, other], axis=0).astype(F32)
+            left = contract_last(one, jnp.concatenate([other, none], axis=0))
+            rest = locals_[p] - (2.0 * shift_ref[p]) * amps_ref[p].astype(F32)
+            results[p] = (rest + jnp.where(lead_ref[p] == 1, lower, left)).astype(BF16)
+        store(k).start()
+        return carry
+
+    lax.fori_loop(0, chunks, body, 0)
+    for k in range(chunks):
+        store(k).wait()
 
 
 SMEM = pl.BlockSpec(memory_space=pltpu.SMEM)
@@ -213,11 +237,11 @@
     tile_bytes = rank * rank * 2
 
     ids = device_base + lax.iota(jnp.int32, pairs)
-    lead = ((ids < mirror) ^ ((ids + mirror) % 2 == 1)).astype(jnp.int32)
+    lead = leads(ids, mirror)
     mirror_owner = (mirror - group_base) // pairs
-    code = jnp.pad(mirror_owner * 2 + lead, (0, LANES - pairs))
-    codes = exchange(jnp.broadcast_to(code[None, None, :], (owners, 1, LANES)))
-    table = codes.reshape(owners * LANES)
+    rows = jnp.broadcast_to(mirror[None, None, :], (owners, 1, pairs))
+    rows = jnp.pad(rows, ((0, 0), (0, 0), (0, LANES - pairs)))
+    table = exchange(rows).reshape(owners * LANES)
 
     projected = call(
         project_kernel,
@@ -233,17 +257,18 @@
     group_dst = edge_dst - group_base
     dst_owner = group_dst // pairs
     dst_slot = group_dst % pairs
+    my_pair_row = lax.dynamic_slice_in_dim(edge_dst, my_owner * edges, edges)
     my_owner_row = lax.dynamic_slice_in_dim(dst_owner, my_owner * edges, edges)
     my_slot_row = lax.dynamic_slice_in_dim(dst_slot, my_owner * edges, edges)
     outgoing = call(
-        couple_kernel,
+        functools.partial(couple_kernel, pairs),
         "couple",
-        [table, my_owner_row * LANES + my_slot_row, my_owner_row, edge_fock],
+        [group_base.reshape(1), table, my_owner_row * LANES + my_slot_row, my_owner_row, my_pair_row, edge_fock],
         [projected, margin],
         pltpu.HBM((owners, rank, rank), BF16),
         HBM,
         2 * edges * rank**3,
-        (2 * edges + owners) * tile_bytes,
+        3 * edges * tile_bytes,
         [pltpu.VMEM((edges, rank, rank), BF16), pltpu.SemaphoreType.DMA((edges, 2))],
     )
     arrived = exchange(outgoing)
@@ -284,60 +309,64 @@
 
     total, direct_row = lax.optimization_barrier((total, direct_row))
 
-    sent, own_sum, mark = call(
+    sent, mark = call(
         sum_kernel,
         "sum",
         [direct_row, turned_row, mirror_owner],
         [arrived],
+        [pltpu.HBM((owners, half, rank), BF16), jax.ShapeDtypeStruct((8, LANES), F32)],
+        [HBM, VMEM],
+        4 * owners * rank**2,
+        (owners + pairs) * tile_bytes,
         [
-            pltpu.HBM((owners, half, rank), BF16),
-            pltpu.HBM((pairs, half, rank), F32),
-            jax.ShapeDtypeStruct((8, LANES), F32),
-        ],
-        [HBM, HBM, VMEM],
-        4 * owners * rank**2,
-        (2 * owners + 2 * pairs) * tile_bytes,
-        [
+            pltpu.VMEM((pairs + 1, half, rank), F32),
             pltpu.VMEM((pairs + 1, half, rank), F32),
             pltpu.VMEM((pairs, half, rank), BF16),
             pltpu.SemaphoreType.DMA((pairs,)),
-            pltpu.SemaphoreType.DMA,
         ],
     )
-    total, fock_pair, mark = lax.optimization_barrier((total, fock_pair, mark))
+    fock_pair = fock_pair + mark[0, 0]
     returned = exchange(sent)
 
+    twice_local, done = call(
+        local_kernel,
+        "local",
+        [lead, mirror_owner, fock_pair],
+        [amps, ints, pno_energy.reshape(pairs, 1, rank), sent],
+        [pltpu.HBM((pairs, rank, rank), F32), jax.ShapeDtypeStruct((8, LANES), F32)],
+        [HBM, VMEM],
+        6 * pairs * rank**2,
+        4 * pairs * tile_bytes,
+        [pltpu.VMEM((pairs, rank, rank), F32), pltpu.SemaphoreType.DMA],
+    )
+    total = total + done
     low, high = own_steps[-2:]
     moved = [swapped(total, "own", step) for step in (low, high, low + high)]
     total = total + moved[0] + (moved[1] + moved[2])
     occ_sums = total.reshape(padded)
     shift = 0.5 * (pick_rows(occ_sums, first_hit) + pick_rows(occ_sums, second_hit))
-    twice_local = call(
-        local_kernel,
-        "local",
-        [fock_pair],
-        [amps, ints, pno_energy.reshape(pairs, 1, rank)],
-        jax.ShapeDtypeStruct((pairs, rank, rank), F32),
-        VMEM,
-        6 * pairs * rank**2,
-        4 * pairs * tile_bytes,
-    )
     return call(
         join_kernel,
         "join",
         [lead, mirror_owner, shift],
-        [returned, own_sum, twice_local, amps],
+        [
+            pltpu.with_memory_space_constraint(returned, pltpu.HBM),
+            pltpu.with_memory_space_constraint(twice_local, pltpu.HBM),
+            amps,
+        ],
         pltpu.HBM((pairs, rank, rank), BF16),
         HBM,
         pairs * rank**2,
         (owners // 2 + 2 * pairs) * tile_bytes,
         [
             pltpu.VMEM((pairs, half, rank), BF16),
+            pltpu.VMEM((pairs, rank, rank), F32),
             pltpu.VMEM((pairs, rank, rank), BF16),
             pltpu.SemaphoreType.DMA((pairs,)),
-            pltpu.SemaphoreType.DMA((pairs,)),
+            pltpu.SemaphoreType.DMA((7,)),
+            pltpu.SemaphoreType.DMA((7,)),
         ],
-        [HBM, VMEM, VMEM, VMEM],
+        [HBM, HBM, VMEM],
     )
 
 

time: 131 us -> 129 us (0.985)
  waiting for transfers between devices: 28.9 us -> 25.8 us
    unnamed x22 -> x24, local copies, waits for them, and re-layouts: 6.14 us -> 3.81 us
    ppermute x10, waiting for transfers between devices: 22 us -> 19.8 us  [swapped(): return lax.ppermute(value, axis, [(i, i ^ step) for i in range(members)])]
  transfers between devices with their start and end apart: 13 -> 13, of which waited for: 12 -> 11; matrix products, arithmetic and copies ran while one was open for 2% -> 4% of each run, Pallas kernels for 3% -> 5%
where the time goes in v3:
time: 129 us; the launch traced here: 128 us
  starting transfers between devices  74.9 us (58%)
  waiting for transfers between devices  25.8 us (20%)
  Pallas kernels  16.9 us (13%)
  local copies, waits for them, and re-layouts  6.56 us (5%)
  other arithmetic  3.37 us (3%)
    ppermute x10, starting transfers between devices, swapped(): return lax.ppermute(value, axis, [(i, i ^ step) for i in range(members)])  46.1 us
    all_to_all x3, starting transfers between devices, exchange(): return lax.all_to_all(tiles, 'own', split_axis=0, concat_axis=0, tiled=True)  28.8 us
    ppermute x10, waiting for transfers between devices, swapped(): return lax.ppermute(value, axis, [(i, i ^ step) for i in range(members)])  19.8 us
    pallas_call x6, Pallas kernels, call(): pl.pallas_call(kernel, in_specs=[SMEM] * len(scalars) + (specs or [VMEM]...  16.9 us
    all_to_all x3, waiting for transfers between devices, exchange(): return lax.all_to_all(tiles, 'own', split_axis=0, concat_axis=0, tiled=True)  6.06 us
    unnamed x24, local copies, waits for them, and re-layouts  3.81 us
  transfers between devices with their start and end apart: 13, of which 11 were waited for; matrix products, arithmetic and copies ran while one was open for 4% of the time, Pallas kernels for 5%

profile of v3, /device:TPU:1, one launch (start us, length us, event | category | flops | bytes accessed | tf_op | source)
XLA Modules:
  0.0 128.0 jit_solution(12635702804827407497)
XLA Ops:
  1.3 11.6 %all-to-all-start = ((s32[64,1,128]{2,1,0:T(1,128)}), s32[64,1,128]{2,1,0:T(1,128)S(1)}, u32[]{:S(2)}, u32[]{:S(2)}) async-start(s32[64,1,128]{2,1,0:T(1,128)} %pad.12), calls=%async_computation | async-start | bytes 65536 | tf_op jit(solution)/shard_map/all_to_all | solution.py:221
  15.2 1.2 copy-done
  16.4 1.4 %copy-done.2 = bf16[48,128,128]{2,1,0:T(8,128)(2,1)S(1)} copy-done((bf16[48,128,128]{2,1,0:T(8,128)(2,1)S(1)}, bf16[48,128,128]{2,1,0:T(8,128)(2,1)}, u32[]{:S(2)}) %copy-start.2) | copy-done | bytes 1572888
  17.8 1.9 %project.1.proj_ref = bf16[48,128,128]{2,1,0:T(8,128)(2,1)S(1)} custom-call(s32[48]{0:T(128)S(1)} %broadcast_subtract_fusion.1.src_ref, bf16[48,128,128]{2,1,0:T(8,128)(2,1)S(1)} %copy-done.2, bf16[28,128,128]{2,1,0:T(8,128)(2,1)S(1)} %copy-done), custom_call_target="tpu_custom_call" | custom-call | flops 201326592 | bytes 4063232 | tf_op jit(solution)/shard_map/project/pallas_call | solution.py:189
  19.7 2.5 %all-to-all-done = s32[64,1,128]{2,1,0:T(1,128)S(1)} async-done(((s32[64,1,128]{2,1,0:T(1,128)}), s32[64,1,128]{2,1,0:T(1,128)S(1)}, u32[]{:S(2)}, u32[]{:S(2)}) %all-to-all-start) | async-done | bytes 32800 | tf_op jit(solution)/shard_map/all_to_all | solution.py:221
  22.2 4.5 %couple.1 = bf16[64,128,128]{2,1,0:T(8,128)(2,1)} custom-call(s32[1]{0:T(128)} %bitcast.3.base_ref, s32[8192]{0:T(1024)S(1)} %bitcast.13, s32[48]{0:T(128)S(1)} %get-tuple-element.22.place_ref, s32[48]{0:T(128)S(1)} %get-tuple-element.23.owner_ref, s32[48]{0:T(128)S(1)} %dynamic_slice.11.pair_ref, f32[48]{0:T(128)S(1)} %copy-done.7, ...), custom_call_target="tpu_custom_call" | custom-call | flops 201326592 | bytes 4718592 | tf_op jit(solution)/shard_map/couple/pallas_call | solution.py:189
  26.8 8.0 %all-to-all-start.1 = ((bf16[64,128,128]{2,1,0:T(8,128)(2,1)}), bf16[64,128,128]{2,1,0:T(8,128)(2,1)S(1)}, u32[]{:S(2)}, u32[]{:S(2)}) async-start(bf16[64,128,128]{2,1,0:T(8,128)(2,1)} %couple.1), calls=%async_computation.1 | async-start | bytes 4194304 | tf_op jit(solution)/shard_map/all_to_all | solution.py:221
  34.8 1.2 copy-done.5
  36.0 0.8 energy.1
  37.4 4.0 %collective-permute-start = (f32[8,128]{1,0:T(8,128)S(1)}, f32[8,128]{1,0:T(8,128)S(1)}, u32[]{:S(2)}, u32[]{:S(2)}) collective-permute-start(f32[8,128]{1,0:T(8,128)S(1)} %bitcast.14), channel_id=1, source_target_pairs={{0,64},{64,0},{128,192},{192,128},{256,320},{320,256},{384,448},{4... | collective-permute-start | bytes 12296 | tf_op jit(solution)/shard_map/ppermute | solution.py:207
  41.4 1.3 collective-permute-done
  42.6 5.8 %collective-permute-start.1 = (f32[8,128]{1,0:T(8,128)S(1)}, f32[8,128]{1,0:T(8,128)S(1)}, u32[]{:S(2)}, u32[]{:S(2)}) collective-permute-start(f32[8,128]{1,0:T(8,128)S(1)} %bitcast_add_fusion), channel_id=1, source_target_pairs={{0,128},{64,192},{128,0},{192,64},{256,384},{320,448},{384,256},{4... | collective-permute-start | bytes 12296 | tf_op jit(solution)/shard_map/ppermute | solution.py:207
  48.6 0.9 collective-permute-done.1
  49.5 8.7 %collective-permute-start.2 = (f32[8,128]{1,0:T(8,128)S(1)}, f32[8,128]{1,0:T(8,128)S(1)}, u32[]{:S(2)}, u32[]{:S(2)}) collective-permute-start(f32[8,128]{1,0:T(8,128)S(1)} %fusion.7), channel_id=1, source_target_pairs={{0,256},{64,320},{128,384},{192,448},{256,0},{320,64},{384,128},{4... | collective-permute-start | bytes 12296 | tf_op jit(solution)/shard_map/ppermute | solution.py:207
  58.3 1.1 collective-permute-done.2
  59.5 4.6 %collective-permute-start.3 = (f32[8,128]{1,0:T(8,128)S(1)}, f32[8,128]{1,0:T(8,128)S(1)}, u32[]{:S(2)}, u32[]{:S(2)}) collective-permute-start(f32[8,128]{1,0:T(8,128)S(1)} %add.111), channel_id=1, source_target_pairs={{0,1},{1,0},{2,3},{3,2},{4,5},{5,4},{6,7},{7,6},{8,9},{9,8},{10,11... | collective-permute-start | bytes 12296 | tf_op jit(solution)/shard_map/ppermute | solution.py:207
  64.1 0.8 collective-permute-done.3
  64.9 3.2 %collective-permute-start.4 = (f32[8,128]{1,0:T(8,128)S(1)}, f32[8,128]{1,0:T(8,128)S(1)}, u32[]{:S(2)}, u32[]{:S(2)}) collective-permute-start(f32[8,128]{1,0:T(8,128)S(1)} %add.112), channel_id=1, source_target_pairs={{0,2},{1,3},{2,0},{3,1},{4,6},{5,7},{6,4},{7,5},{8,10},{9,11},{10,... | collective-permute-start | bytes 12296 | tf_op jit(solution)/shard_map/ppermute | solution.py:207
  68.2 1.4 %collective-permute-done.4 = f32[8,128]{1,0:T(8,128)S(1)} collective-permute-done((f32[8,128]{1,0:T(8,128)S(1)}, f32[8,128]{1,0:T(8,128)S(1)}, u32[]{:S(2)}, u32[]{:S(2)}) %collective-permute-start.4) | collective-permute-done | bytes 4128 | tf_op jit(solution)/shard_map/ppermute | solution.py:207
  69.6 4.7 %collective-permute-start.5 = (f32[8,128]{1,0:T(8,128)S(1)}, f32[8,128]{1,0:T(8,128)S(1)}, u32[]{:S(2)}, u32[]{:S(2)}) collective-permute-start(f32[8,128]{1,0:T(8,128)S(1)} %add.113), channel_id=1, source_target_pairs={{0,4},{1,5},{2,6},{3,7},{4,0},{5,1},{6,2},{7,3},{8,12},{9,13},{10,... | collective-permute-start | bytes 12296 | tf_op jit(solution)/shard_map/ppermute | solution.py:207
  74.6 1.2 collective-permute-done.5
  75.8 3.6 %collective-permute-start.6 = (f32[8,128]{1,0:T(8,128)S(1)}, f32[8,128]{1,0:T(8,128)S(1)}, u32[]{:S(2)}, u32[]{:S(2)}) collective-permute-start(f32[8,128]{1,0:T(8,128)S(1)} %add.114), channel_id=1, source_target_pairs={{0,8},{1,9},{2,10},{3,11},{4,12},{5,13},{6,14},{7,15},{8,0},{9,1},... | collective-permute-start | bytes 12296 | tf_op jit(solution)/shard_map/ppermute | solution.py:207
  79.4 2.1 %collective-permute-done.6 = f32[8,128]{1,0:T(8,128)S(1)} collective-permute-done((f32[8,128]{1,0:T(8,128)S(1)}, f32[8,128]{1,0:T(8,128)S(1)}, u32[]{:S(2)}, u32[]{:S(2)}) %collective-permute-start.6) | collective-permute-done | bytes 4128 | tf_op jit(solution)/shard_map/ppermute | solution.py:207
  81.4 3.0 %all-to-all-done.1.arrived_ref = bf16[64,128,128]{2,1,0:T(8,128)(2,1)S(1)} async-done(((bf16[64,128,128]{2,1,0:T(8,128)(2,1)}), bf16[64,128,128]{2,1,0:T(8,128)(2,1)S(1)}, u32[]{:S(2)}, u32[]{:S(2)}) %all-to-all-start.1) | async-done | bytes 2097184 | tf_op jit(solution)/shard_map/all_to_all | solution.py:221
  84.4 2.2 %sum.1 = (bf16[64,64,128]{2,1,0:T(8,128)(2,1)}, f32[8,128]{1,0:T(8,128)S(1)}) custom-call(s32[64]{0:T(128)S(1)} %compare_select_fusion.3.direct_ref, s32[64]{0:T(128)S(1)} %compare_select_fusion.2.turned_ref, s32[28]{0:T(128)S(1)} %get-tuple-element.26.target_ref, bf16[64,128,128]{2,1,0:T(8,128)(2,1)S(1)} %all-to-all-done.1.arrived_ref), custom_call_target="tpu_custom_call" | custom-call | flops 4194304 | bytes 3014656 | tf_op jit(solution)/shard_map/sum/pallas_call | solution.py:189
  86.7 9.2 %all-to-all-start.2 = ((bf16[64,64,128]{2,1,0:T(8,128)(2,1)}), bf16[64,64,128]{2,1,0:T(8,128)(2,1)}, u32[]{:S(2)}, u32[]{:S(2)}) async-start(bf16[64,64,128]{2,1,0:T(8,128)(2,1)} %get-tuple-element.14.sent_ref), calls=%async_computation.2 | async-start | bytes 2097152 | tf_op jit(solution)/shard_map/all_to_all | solution.py:221
  97.2 3.4 %local.1 = (f32[28,128,128]{2,1,0:T(8,128)}, f32[8,128]{1,0:T(8,128)S(1)}) custom-call(s32[28]{0:T(128)S(1)} %xor_convert_fusion.lead_ref, s32[28]{0:T(128)S(1)} %get-tuple-element.26.target_ref, f32[28]{0:T(128)S(1)} %add_add_fusion.fock_ref, bf16[28,128,128]{2,1,0:T(8,128)(2,1)S(1)} %copy-done.1, bf16[28,128,128]{2,1,0:T(8,128)(2,1)S(1)} %copy-done.6, ...), custom_call_target="tpu_custom_call" | custom-call | flops 2752512 | bytes 3670016 | tf_op jit(solution)/shard_map/local/pallas_call | solution.py:189
  100.6 7.3 %collective-permute-start.8 = (f32[8,128]{1,0:T(8,128)S(1)}, f32[8,128]{1,0:T(8,128)S(1)}, u32[]{:S(2)}, u32[]{:S(2)}) collective-permute-start(f32[8,128]{1,0:T(8,128)S(1)} %add.125), channel_id=1, source_target_pairs={{0,32},{1,33},{2,34},{3,35},{4,36},{5,37},{6,38},{7,39},{8,40},{9,... | collective-permute-start | bytes 12296 | tf_op jit(solution)/shard_map/ppermute | solution.py:207
  107.9 2.1 %collective-permute-start.9 = (f32[8,128]{1,0:T(8,128)S(1)}, f32[8,128]{1,0:T(8,128)S(1)}, u32[]{:S(2)}, u32[]{:S(2)}) collective-permute-start(f32[8,128]{1,0:T(8,128)S(1)} %add.125), channel_id=1, source_target_pairs={{0,48},{1,49},{2,50},{3,51},{4,52},{5,53},{6,54},{7,55},{8,56},{9,... | collective-permute-start | bytes 12296 | tf_op jit(solution)/shard_map/ppermute | solution.py:207
  110.0 2.1 %collective-permute-start.7 = (f32[8,128]{1,0:T(8,128)S(1)}, f32[8,128]{1,0:T(8,128)S(1)}, u32[]{:S(2)}, u32[]{:S(2)}) collective-permute-start(f32[8,128]{1,0:T(8,128)S(1)} %add.125), channel_id=1, source_target_pairs={{0,16},{1,17},{2,18},{3,19},{4,20},{5,21},{6,22},{7,23},{8,24},{9,... | collective-permute-start | bytes 12296 | tf_op jit(solution)/shard_map/ppermute | solution.py:207
  112.1 11.1 %collective-permute-done.8 = f32[8,128]{1,0:T(8,128)S(1)} collective-permute-done((f32[8,128]{1,0:T(8,128)S(1)}, f32[8,128]{1,0:T(8,128)S(1)}, u32[]{:S(2)}, u32[]{:S(2)}) %collective-permute-start.8) | collective-permute-done | bytes 4128 | tf_op jit(solution)/shard_map/ppermute | solution.py:207
  123.9 4.0 %join.1 = bf16[28,128,128]{2,1,0:T(8,128)(2,1)} custom-call(s32[28]{0:T(128)S(1)} %xor_convert_fusion.lead_ref, s32[28]{0:T(128)S(1)} %get-tuple-element.26.target_ref, f32[28]{0:T(128)S(1)} %add_multiply_fusion.shift_ref, bf16[64,64,128]{2,1,0:T(8,128)(2,1)} %all-to-all-done.2.returned_ref, f32[28,128,128]{2,1,0:T(8,128)} %get-tuple-element.16.local_ref, ...), custom_call_target="tpu_custom_call" | custom-call | flops 458752 | bytes 2883584 | tf_op jit(solution)/shard_map/join/pallas_call | solution.py:189
  (58 shorter events, 6.7 us)
Async XLA Ops:
  1.3 20.9 %all-to-all-start = ((s32[64,1,128]{2,1,0:T(1,128)}), s32[64,1,128]{2,1,0:T(1,128)S(1)}, u32[]{:S(2)}, u32[]{:S(2)}) async-start(s32[64,1,128]{2,1,0:T(1,128)} %pad.12), calls=%async_computation | async-start | bytes 65536 | tf_op jit(solution)/shard_map/all_to_all | solution.py:221
  15.2 1.2 copy-start
  16.4 1.4 %copy-start.2 = (bf16[48,128,128]{2,1,0:T(8,128)(2,1)S(1)}, bf16[48,128,128]{2,1,0:T(8,128)(2,1)}, u32[]{:S(2)}) copy-start(bf16[48,128,128]{2,1,0:T(8,128)(2,1)} %margin_ref.3) | copy-start | bytes 4718596
  17.8 4.5 %copy-start.3 = (bf16[48,128,128]{2,1,0:T(8,128)(2,1)S(1)}, bf16[48,128,128]{2,1,0:T(8,128)(2,1)}, u32[]{:S(2)}) copy-start(bf16[48,128,128]{2,1,0:T(8,128)(2,1)} %margin_ref.3) | copy-start | bytes 4718596
  17.8 4.5 %copy-start.7 = (f32[48]{0:T(128)S(1)}, f32[48]{0:T(128)}, u32[]{:S(2)}) copy-start(f32[48]{0:T(128)} %fock_ref.1) | copy-start | bytes 580
  26.7 8.0 %copy-start.9 = (f32[1000]{0:T(1024)S(1)}, f32[1000]{0:T(1024)}, u32[]{:S(2)}) copy-start(f32[1000]{0:T(1024)} %param.13) | copy-start | bytes 12004
  26.8 8.0 %copy-start.1 = (bf16[28,128,128]{2,1,0:T(8,128)(2,1)S(1)}, bf16[28,128,128]{2,1,0:T(8,128)(2,1)}, u32[]{:S(2)}) copy-start(bf16[28,128,128]{2,1,0:T(8,128)(2,1)} %amps_ref.7) | copy-start | bytes 2752516
  26.8 57.7 %all-to-all-start.1 = ((bf16[64,128,128]{2,1,0:T(8,128)(2,1)}), bf16[64,128,128]{2,1,0:T(8,128)(2,1)S(1)}, u32[]{:S(2)}, u32[]{:S(2)}) async-start(bf16[64,128,128]{2,1,0:T(8,128)(2,1)} %couple.1), calls=%async_computation.1 | async-start | bytes 4194304 | tf_op jit(solution)/shard_map/all_to_all | solution.py:221
  34.7 2.4 %copy-start.10 = (s32[2,28]{1,0:T(2,128)S(1)}, s32[2,28]{1,0:T(2,128)}, u32[]{:S(2)}) copy-start(s32[2,28]{1,0:T(2,128)} %param.14) | copy-start | bytes 676
  34.8 13.7 %copy-start.11 = (s32[28]{0:T(128)S(1)}, s32[28]{0:T(128)}, u32[]{:S(2)}) copy-start(s32[28]{0:T(128)} %param.15) | copy-start | bytes 340
  34.8 1.2 copy-start.5
  37.4 5.3 %collective-permute-start = (f32[8,128]{1,0:T(8,128)S(1)}, f32[8,128]{1,0:T(8,128)S(1)}, u32[]{:S(2)}, u32[]{:S(2)}) collective-permute-start(f32[8,128]{1,0:T(8,128)S(1)} %bitcast.14), channel_id=1, source_target_pairs={{0,64},{64,0},{128,192},{192,128},{256,320},{320,256},{384,448},{4... | collective-permute-start | bytes 12296 | tf_op jit(solution)/shard_map/ppermute | solution.py:207
  42.6 6.8 %collective-permute-start.1 = (f32[8,128]{1,0:T(8,128)S(1)}, f32[8,128]{1,0:T(8,128)S(1)}, u32[]{:S(2)}, u32[]{:S(2)}) collective-permute-start(f32[8,128]{1,0:T(8,128)S(1)} %bitcast_add_fusion), channel_id=1, source_target_pairs={{0,128},{64,192},{128,0},{192,64},{256,384},{320,448},{384,256},{4... | collective-permute-start | bytes 12296 | tf_op jit(solution)/shard_map/ppermute | solution.py:207
  49.5 10.0 %collective-permute-start.2 = (f32[8,128]{1,0:T(8,128)S(1)}, f32[8,128]{1,0:T(8,128)S(1)}, u32[]{:S(2)}, u32[]{:S(2)}) collective-permute-start(f32[8,128]{1,0:T(8,128)S(1)} %fusion.7), channel_id=1, source_target_pairs={{0,256},{64,320},{128,384},{192,448},{256,0},{320,64},{384,128},{4... | collective-permute-start | bytes 12296 | tf_op jit(solution)/shard_map/ppermute | solution.py:207
  59.5 5.4 %collective-permute-start.3 = (f32[8,128]{1,0:T(8,128)S(1)}, f32[8,128]{1,0:T(8,128)S(1)}, u32[]{:S(2)}, u32[]{:S(2)}) collective-permute-start(f32[8,128]{1,0:T(8,128)S(1)} %add.111), channel_id=1, source_target_pairs={{0,1},{1,0},{2,3},{3,2},{4,5},{5,4},{6,7},{7,6},{8,9},{9,8},{10,11... | collective-permute-start | bytes 12296 | tf_op jit(solution)/shard_map/ppermute | solution.py:207
  64.9 4.6 %collective-permute-start.4 = (f32[8,128]{1,0:T(8,128)S(1)}, f32[8,128]{1,0:T(8,128)S(1)}, u32[]{:S(2)}, u32[]{:S(2)}) collective-permute-start(f32[8,128]{1,0:T(8,128)S(1)} %add.112), channel_id=1, source_target_pairs={{0,2},{1,3},{2,0},{3,1},{4,6},{5,7},{6,4},{7,5},{8,10},{9,11},{10,... | collective-permute-start | bytes 12296 | tf_op jit(solution)/shard_map/ppermute | solution.py:207
  69.6 6.2 %collective-permute-start.5 = (f32[8,128]{1,0:T(8,128)S(1)}, f32[8,128]{1,0:T(8,128)S(1)}, u32[]{:S(2)}, u32[]{:S(2)}) collective-permute-start(f32[8,128]{1,0:T(8,128)S(1)} %add.113), channel_id=1, source_target_pairs={{0,4},{1,5},{2,6},{3,7},{4,0},{5,1},{6,2},{7,3},{8,12},{9,13},{10,... | collective-permute-start | bytes 12296 | tf_op jit(solution)/shard_map/ppermute | solution.py:207
  75.8 5.6 %collective-permute-start.6 = (f32[8,128]{1,0:T(8,128)S(1)}, f32[8,128]{1,0:T(8,128)S(1)}, u32[]{:S(2)}, u32[]{:S(2)}) collective-permute-start(f32[8,128]{1,0:T(8,128)S(1)} %add.114), channel_id=1, source_target_pairs={{0,8},{1,9},{2,10},{3,11},{4,12},{5,13},{6,14},{7,15},{8,0},{9,1},... | collective-permute-start | bytes 12296 | tf_op jit(solution)/shard_map/ppermute | solution.py:207
  84.4 11.5 %copy-start.8 = (f32[28,128]{1,0:T(8,128)S(1)}, f32[28,128]{1,0:T(8,128)}, u32[]{:S(2)}) copy-start(f32[28,128]{1,0:T(8,128)} %param.12) | copy-start | bytes 43012
  86.7 10.5 %copy-start.4 = (bf16[64,64,128]{2,1,0:T(8,128)(2,1)S(1)}, bf16[64,64,128]{2,1,0:T(8,128)(2,1)}, u32[]{:S(2)}) copy-start(bf16[64,64,128]{2,1,0:T(8,128)(2,1)} %get-tuple-element.14.sent_ref) | copy-start | bytes 3145732
  86.7 10.5 %copy-start.6 = (bf16[28,128,128]{2,1,0:T(8,128)(2,1)S(1)}, bf16[28,128,128]{2,1,0:T(8,128)(2,1)}, u32[]{:S(2)}) copy-start(bf16[28,128,128]{2,1,0:T(8,128)(2,1)} %ints_ref.3) | copy-start | bytes 2752516
  86.7 37.2 %all-to-all-start.2 = ((bf16[64,64,128]{2,1,0:T(8,128)(2,1)}), bf16[64,64,128]{2,1,0:T(8,128)(2,1)}, u32[]{:S(2)}, u32[]{:S(2)}) async-start(bf16[64,64,128]{2,1,0:T(8,128)(2,1)} %get-tuple-element.14.sent_ref), calls=%async_computation.2 | async-start | bytes 2097152 | tf_op jit(solution)/shard_map/all_to_all | solution.py:221
  100.6 22.6 %collective-permute-start.8 = (f32[8,128]{1,0:T(8,128)S(1)}, f32[8,128]{1,0:T(8,128)S(1)}, u32[]{:S(2)}, u32[]{:S(2)}) collective-permute-start(f32[8,128]{1,0:T(8,128)S(1)} %add.125), channel_id=1, source_target_pairs={{0,32},{1,33},{2,34},{3,35},{4,36},{5,37},{6,38},{7,39},{8,40},{9,... | collective-permute-start | bytes 12296 | tf_op jit(solution)/shard_map/ppermute | solution.py:207
  107.9 15.3 %collective-permute-start.9 = (f32[8,128]{1,0:T(8,128)S(1)}, f32[8,128]{1,0:T(8,128)S(1)}, u32[]{:S(2)}, u32[]{:S(2)}) collective-permute-start(f32[8,128]{1,0:T(8,128)S(1)} %add.125), channel_id=1, source_target_pairs={{0,48},{1,49},{2,50},{3,51},{4,52},{5,53},{6,54},{7,55},{8,56},{9,... | collective-permute-start | bytes 12296 | tf_op jit(solution)/shard_map/ppermute | solution.py:207
  110.0 13.2 %collective-permute-start.7 = (f32[8,128]{1,0:T(8,128)S(1)}, f32[8,128]{1,0:T(8,128)S(1)}, u32[]{:S(2)}, u32[]{:S(2)}) collective-permute-start(f32[8,128]{1,0:T(8,128)S(1)} %add.125), channel_id=1, source_target_pairs={{0,16},{1,17},{2,18},{3,19},{4,20},{5,21},{6,22},{7,23},{8,24},{9,... | collective-permute-start | bytes 12296 | tf_op jit(solution)/shard_map/ppermute | solution.py:207

commit v4 on v3

--- a/solution.py
+++ b/solution.py
@@ -17,13 +17,31 @@
     return lax.dot_general(left, right, (((1,), (1,)), ((), ())), preferred_element_type=F32)
 
 
-def project_kernel(src_ref, margin_ref, amps_ref, out_ref):
-    def body(e, carry):
-        tile = amps_ref[src_ref[e]]
-        out_ref[e] = jnp.dot(margin_ref[e], tile, preferred_element_type=F32).astype(BF16)
-        return carry
-
-    lax.fori_loop(0, margin_ref.shape[0], body, 0, unroll=8)
+def project_kernel(src_ref, margin_ref, amps_ref, out_ref, margins, tiles, margin_sems, tile_sems):
+    edges, pairs = margins.shape[0], tiles.shape[0]
+    chunks = margin_sems.shape[0]
+    count = edges // chunks
+    base = (lax.axis_index("grp") * lax.axis_size("own") + lax.axis_index("own")) * pairs
+
+    def load(k):
+        rows = pl.ds(k * count, count)
+        return pltpu.make_async_copy(margin_ref.at[rows], margins.at[rows], margin_sems.at[k])
+
+    every = pltpu.make_async_copy(amps_ref, tiles, tile_sems)
+    every.start()
+    for k in range(chunks):
+        load(k).start()
+    every.wait()
+
+    def body(k, carry):
+        load(k).wait()
+        for i in range(count):
+            e = k * count + i
+            tile = tiles[src_ref[e] - base]
+            out_ref[e] = jnp.dot(margins[e], tile, preferred_element_type=F32).astype(BF16)
+        return carry
+
+    lax.fori_loop(0, chunks, body, 0)
 
 
 def energy_kernel(amps_ref, ints_ref, out_ref):
@@ -40,44 +58,36 @@
     return ((pair < other) ^ ((pair + other) % 2 == 1)).astype(jnp.int32)
 
 
-def couple_kernel(pairs, base_ref, table_ref, place_ref, owner_ref, pair_ref, fock_ref, proj_ref, margin_ref, out_ref, tiles, sems):
-    edges = tiles.shape[0]
-    half = tiles.shape[1] // 2
+def couple_kernel(pairs, table_ref, dst_ref, fock_ref, proj_ref, margin_ref, out_ref, slots, sem):
+    edges = proj_ref.shape[0]
+    half = proj_ref.shape[1] // 2
     scale = -(-(1 << 20) // pairs)
-    reach = pairs * out_ref.shape[0]
+    owners = out_ref.shape[0]
+    reach = pairs * owners
+    base = lax.axis_index("grp") * reach
+    first = lax.axis_index("own") * edges
     assert all(x * scale >> 20 == x // pairs for x in range(reach)) and reach * scale < 2**31
 
-    def copies(e, other):
-        direct = pltpu.make_async_copy(
-            tiles.at[e, pl.ds(0, half)], out_ref.at[owner_ref[e], pl.ds(0, half)], sems.at[e, 0]
-        )
-        turned = pltpu.make_async_copy(
-            tiles.at[e, pl.ds(half, half)], out_ref.at[other, pl.ds(half, half)], sems.at[e, 1]
-        )
-        return direct, turned
-
-    def start(e, carry):
-        twin = table_ref[place_ref[e]]
-        pair = pair_ref[e]
+    def place(e, carry):
+        pair = dst_ref[first + e]
+        owner = ((pair - base) * scale) >> 20
+        twin = table_ref[owner * LANES + (pair - base - owner * pairs)]
         lead = (((pair < twin).astype(jnp.int32) + pair + twin) & 1) == 1
-        other = ((twin - base_ref[0]) * scale) >> 20
+        other = ((twin - base) * scale) >> 20
         proj = proj_ref[e]
         marg = margin_ref[e]
         turned = jnp.concatenate([marg[half:], marg[:half]], axis=0)
         left = jnp.where(lead, proj, turned)
         right = jnp.where(lead, marg, proj)
-        tiles[e] = (contract_last(left, right) * fock_ref[e]).astype(BF16)
-        for copy in copies(e, other):
-            copy.start()
-        return carry
-
-    def finish(e, carry):
-        for copy in copies(e, 0):
-            copy.wait()
-        return carry
-
-    lax.fori_loop(0, edges, start, 0, unroll=8)
-    lax.fori_loop(0, edges, finish, 0, unroll=8)
+        tile = (contract_last(left, right) * fock_ref[e]).astype(BF16)
+        slots[owner, :half, :] = tile[:half]
+        slots[other, half:, :] = tile[half:]
+        return carry
+
+    lax.fori_loop(0, edges, place, 0, unroll=8)
+    copy = pltpu.make_async_copy(slots, out_ref, sem)
+    copy.start()
+    copy.wait()
 
 
 def sum_kernel(direct_ref, turned_ref, target_ref, arrived_ref, sent_ref, mark_ref, direct_acc, turned_acc, tiles, sems):
@@ -246,30 +256,35 @@
     projected = call(
         project_kernel,
         "project",
-        [edge_src - device_base],
-        [margin, amps],
+        [edge_src],
+        [
+            pltpu.with_memory_space_constraint(margin, pltpu.HBM),
+            pltpu.with_memory_space_constraint(amps, pltpu.HBM),
+        ],
         jax.ShapeDtypeStruct((edges, rank, rank), BF16),
         VMEM,
         2 * edges * rank**3,
         (2 * edges + pairs) * tile_bytes,
+        [
+            pltpu.VMEM((edges, rank, rank), BF16),
+            pltpu.VMEM((pairs, rank, rank), BF16),
+            pltpu.SemaphoreType.DMA((6,)),
+            pltpu.SemaphoreType.DMA,
+        ],
+        [HBM, HBM],
     )
 
     group_dst = edge_dst - group_base
-    dst_owner = group_dst // pairs
-    dst_slot = group_dst % pairs
-    my_pair_row = lax.dynamic_slice_in_dim(edge_dst, my_owner * edges, edges)
-    my_owner_row = lax.dynamic_slice_in_dim(dst_owner, my_owner * edges, edges)
-    my_slot_row = lax.dynamic_slice_in_dim(dst_slot, my_owner * edges, edges)
     outgoing = call(
         functools.partial(couple_kernel, pairs),
         "couple",
-        [group_base.reshape(1), table, my_owner_row * LANES + my_slot_row, my_owner_row, my_pair_row, edge_fock],
+        [table, edge_dst, edge_fock],
         [projected, margin],
         pltpu.HBM((owners, rank, rank), BF16),
         HBM,
         2 * edges * rank**3,
         3 * edges * tile_bytes,
-        [pltpu.VMEM((edges, rank, rank), BF16), pltpu.SemaphoreType.DMA((edges, 2))],
+        [pltpu.VMEM((owners, rank, rank), BF16), pltpu.SemaphoreType.DMA],
     )
     arrived = exchange(outgoing)
 

time: 129 us -> 126 us (0.977)
  starting transfers between devices: 74.9 us -> 71.8 us
  waiting for transfers between devices: 25.8 us -> 28.8 us
  local copies, waits for them, and re-layouts: 6.56 us -> 3.84 us
  Pallas kernels: 16.9 us -> 18.6 us
  other arithmetic: 3.37 us -> 1.9 us
    all_to_all x3, starting transfers between devices: 28.8 us -> 26.1 us  [exchange(): return lax.all_to_all(tiles, 'own', split_axis=0, concat_axis=0, tiled=True)]
    all_to_all x3, waiting for transfers between devices: 6.06 us -> 8.64 us  [exchange(): return lax.all_to_all(tiles, 'own', split_axis=0, concat_axis=0, tiled=True)]
    unnamed x24, local copies, waits for them, and re-layouts: 3.81 us -> 1.88 us
    pallas_call x6, Pallas kernels: 16.9 us -> 18.6 us  [call(): pl.pallas_call(kernel, in_specs=[SMEM] * len(scalars) + (specs or [VMEM]...]
  transfers between devices with their start and end apart: 13 -> 13, of which waited for: 11 -> 11; matrix products, arithmetic and copies ran while one was open for 4% -> 2% of each run, Pallas kernels for 5% -> 6%
where the time goes in v4:
time: 126 us; the launch traced here: 125 us
  starting transfers between devices  71.8 us (57%)
  waiting for transfers between devices  28.8 us (23%)
  Pallas kernels  18.6 us (15%)
  local copies, waits for them, and re-layouts  3.84 us (3%)
  other arithmetic  1.9 us (2%)
    ppermute x10, starting transfers between devices, swapped(): return lax.ppermute(value, axis, [(i, i ^ step) for i in range(members)])  45.7 us
    all_to_all x3, starting transfers between devices, exchange(): return lax.all_to_all(tiles, 'own', split_axis=0, concat_axis=0, tiled=True)  26.1 us
    ppermute x10, waiting for transfers between devices, swapped(): return lax.ppermute(value, axis, [(i, i ^ step) for i in range(members)])  20.2 us
    pallas_call x6, Pallas kernels, call(): pl.pallas_call(kernel, in_specs=[SMEM] * len(scalars) + (specs or [VMEM]...  18.6 us
    all_to_all x3, waiting for transfers between devices, exchange(): return lax.all_to_all(tiles, 'own', split_axis=0, concat_axis=0, tiled=True)  8.64 us
  transfers between devices with their start and end apart: 13, of which 11 were waited for; matrix products, arithmetic and copies ran while one was open for 2% of the time, Pallas kernels for 6%

profile of v4, /device:TPU:1, one launch (start us, length us, event | category | flops | bytes accessed | tf_op | source)
XLA Modules:
  0.0 125.4 jit_solution(16786918204878574146)
XLA Ops:
  0.0 0.7 pad.11
  1.3 11.6 %all-to-all-start = ((s32[64,1,128]{2,1,0:T(1,128)}), s32[64,1,128]{2,1,0:T(1,128)S(1)}, u32[]{:S(2)}, u32[]{:S(2)}) async-start(s32[64,1,128]{2,1,0:T(1,128)} %pad.12), calls=%async_computation | async-start | bytes 65536 | tf_op jit(solution)/shard_map/all_to_all | solution.py:231
  13.6 3.5 %project.1.proj_ref = bf16[48,128,128]{2,1,0:T(8,128)(2,1)S(1)} custom-call(s32[48]{0:T(128)S(1)} %copy-done.6, bf16[48,128,128]{2,1,0:T(8,128)(2,1)} %margin_ref.3, bf16[28,128,128]{2,1,0:T(8,128)(2,1)} %amps_ref.7), custom_call_target="tpu_custom_call" | custom-call | flops 201326592 | bytes 4063232 | tf_op jit(solution)/shard_map/project/pallas_call | solution.py:199
  17.1 5.1 %all-to-all-done = s32[64,1,128]{2,1,0:T(1,128)S(1)} async-done(((s32[64,1,128]{2,1,0:T(1,128)}), s32[64,1,128]{2,1,0:T(1,128)S(1)}, u32[]{:S(2)}, u32[]{:S(2)}) %all-to-all-start) | async-done | bytes 32800 | tf_op jit(solution)/shard_map/all_to_all | solution.py:231
  22.3 4.6 %couple.1 = bf16[64,128,128]{2,1,0:T(8,128)(2,1)} custom-call(s32[8192]{0:T(1024)S(1)} %bitcast.12, s32[3072]{0:T(1024)S(1)} %copy-done.5, f32[48]{0:T(128)S(1)} %copy-done.7, bf16[48,128,128]{2,1,0:T(8,128)(2,1)S(1)} %project.1.proj_ref, bf16[48,128,128]{2,1,0:T(8,128)(2,1)S(1)} %copy-done.1), custom_call_target="tpu_custom_call" | custom-call | flops 201326592 | bytes 4718592 | tf_op jit(solution)/shard_map/couple/pallas_call | solution.py:199
  26.8 5.3 %all-to-all-start.1 = ((bf16[64,128,128]{2,1,0:T(8,128)(2,1)}), bf16[64,128,128]{2,1,0:T(8,128)(2,1)S(1)}, u32[]{:S(2)}, u32[]{:S(2)}) async-start(bf16[64,128,128]{2,1,0:T(8,128)(2,1)} %couple.1), calls=%async_computation.1 | async-start | bytes 4194304 | tf_op jit(solution)/shard_map/all_to_all | solution.py:231
  32.3 1.2 copy-done.3
  33.4 0.8 energy.1
  34.8 4.0 %collective-permute-start = (f32[8,128]{1,0:T(8,128)S(1)}, f32[8,128]{1,0:T(8,128)S(1)}, u32[]{:S(2)}, u32[]{:S(2)}) collective-permute-start(f32[8,128]{1,0:T(8,128)S(1)} %bitcast.13), channel_id=1, source_target_pairs={{0,64},{64,0},{128,192},{192,128},{256,320},{320,256},{384,448},{4... | collective-permute-start | bytes 12296 | tf_op jit(solution)/shard_map/ppermute | solution.py:217
  38.9 1.3 %collective-permute-done = f32[8,128]{1,0:T(8,128)S(1)} collective-permute-done((f32[8,128]{1,0:T(8,128)S(1)}, f32[8,128]{1,0:T(8,128)S(1)}, u32[]{:S(2)}, u32[]{:S(2)}) %collective-permute-start) | collective-permute-done | bytes 4128 | tf_op jit(solution)/shard_map/ppermute | solution.py:217
  40.1 5.8 %collective-permute-start.1 = (f32[8,128]{1,0:T(8,128)S(1)}, f32[8,128]{1,0:T(8,128)S(1)}, u32[]{:S(2)}, u32[]{:S(2)}) collective-permute-start(f32[8,128]{1,0:T(8,128)S(1)} %bitcast_add_fusion), channel_id=1, source_target_pairs={{0,128},{64,192},{128,0},{192,64},{256,384},{320,448},{384,256},{4... | collective-permute-start | bytes 12296 | tf_op jit(solution)/shard_map/ppermute | solution.py:217
  46.0 0.9 collective-permute-done.1
  46.9 8.7 %collective-permute-start.2 = (f32[8,128]{1,0:T(8,128)S(1)}, f32[8,128]{1,0:T(8,128)S(1)}, u32[]{:S(2)}, u32[]{:S(2)}) collective-permute-start(f32[8,128]{1,0:T(8,128)S(1)} %fusion.6), channel_id=1, source_target_pairs={{0,256},{64,320},{128,384},{192,448},{256,0},{320,64},{384,128},{4... | collective-permute-start | bytes 12296 | tf_op jit(solution)/shard_map/ppermute | solution.py:217
  55.8 1.1 collective-permute-done.2
  56.9 4.6 %collective-permute-start.3 = (f32[8,128]{1,0:T(8,128)S(1)}, f32[8,128]{1,0:T(8,128)S(1)}, u32[]{:S(2)}, u32[]{:S(2)}) collective-permute-start(f32[8,128]{1,0:T(8,128)S(1)} %add.96), channel_id=1, source_target_pairs={{0,1},{1,0},{2,3},{3,2},{4,5},{5,4},{6,7},{7,6},{8,9},{9,8},{10,11... | collective-permute-start | bytes 12296 | tf_op jit(solution)/shard_map/ppermute | solution.py:217
  61.6 0.8 collective-permute-done.3
  62.4 3.2 %collective-permute-start.4 = (f32[8,128]{1,0:T(8,128)S(1)}, f32[8,128]{1,0:T(8,128)S(1)}, u32[]{:S(2)}, u32[]{:S(2)}) collective-permute-start(f32[8,128]{1,0:T(8,128)S(1)} %add.97), channel_id=1, source_target_pairs={{0,2},{1,3},{2,0},{3,1},{4,6},{5,7},{6,4},{7,5},{8,10},{9,11},{10,... | collective-permute-start | bytes 12296 | tf_op jit(solution)/shard_map/ppermute | solution.py:217
  65.7 1.4 %collective-permute-done.4 = f32[8,128]{1,0:T(8,128)S(1)} collective-permute-done((f32[8,128]{1,0:T(8,128)S(1)}, f32[8,128]{1,0:T(8,128)S(1)}, u32[]{:S(2)}, u32[]{:S(2)}) %collective-permute-start.4) | collective-permute-done | bytes 4128 | tf_op jit(solution)/shard_map/ppermute | solution.py:217
  67.0 4.7 %collective-permute-start.5 = (f32[8,128]{1,0:T(8,128)S(1)}, f32[8,128]{1,0:T(8,128)S(1)}, u32[]{:S(2)}, u32[]{:S(2)}) collective-permute-start(f32[8,128]{1,0:T(8,128)S(1)} %add.98), channel_id=1, source_target_pairs={{0,4},{1,5},{2,6},{3,7},{4,0},{5,1},{6,2},{7,3},{8,12},{9,13},{10,... | collective-permute-start | bytes 12296 | tf_op jit(solution)/shard_map/ppermute | solution.py:217
  72.0 1.2 collective-permute-done.5
  73.3 3.1 %collective-permute-start.6 = (f32[8,128]{1,0:T(8,128)S(1)}, f32[8,128]{1,0:T(8,128)S(1)}, u32[]{:S(2)}, u32[]{:S(2)}) collective-permute-start(f32[8,128]{1,0:T(8,128)S(1)} %add.99), channel_id=1, source_target_pairs={{0,8},{1,9},{2,10},{3,11},{4,12},{5,13},{6,14},{7,15},{8,0},{9,1},... | collective-permute-start | bytes 12296 | tf_op jit(solution)/shard_map/ppermute | solution.py:217
  76.4 2.5 %collective-permute-done.6 = f32[8,128]{1,0:T(8,128)S(1)} collective-permute-done((f32[8,128]{1,0:T(8,128)S(1)}, f32[8,128]{1,0:T(8,128)S(1)}, u32[]{:S(2)}, u32[]{:S(2)}) %collective-permute-start.6) | collective-permute-done | bytes 4128 | tf_op jit(solution)/shard_map/ppermute | solution.py:217
  78.9 3.0 %all-to-all-done.1.arrived_ref = bf16[64,128,128]{2,1,0:T(8,128)(2,1)S(1)} async-done(((bf16[64,128,128]{2,1,0:T(8,128)(2,1)}), bf16[64,128,128]{2,1,0:T(8,128)(2,1)S(1)}, u32[]{:S(2)}, u32[]{:S(2)}) %all-to-all-start.1) | async-done | bytes 2097184 | tf_op jit(solution)/shard_map/all_to_all | solution.py:231
  81.9 2.2 %sum.1 = (bf16[64,64,128]{2,1,0:T(8,128)(2,1)}, f32[8,128]{1,0:T(8,128)S(1)}) custom-call(s32[64]{0:T(128)S(1)} %compare_select_fusion.3.direct_ref, s32[64]{0:T(128)S(1)} %compare_select_fusion.2.turned_ref, s32[28]{0:T(128)S(1)} %get-tuple-element.22.target_ref, bf16[64,128,128]{2,1,0:T(8,128)(2,1)S(1)} %all-to-all-done.1.arrived_ref), custom_call_target="tpu_custom_call" | custom-call | flops 4194304 | bytes 3014656 | tf_op jit(solution)/shard_map/sum/pallas_call | solution.py:199
  84.1 9.2 %all-to-all-start.2 = ((bf16[64,64,128]{2,1,0:T(8,128)(2,1)}), bf16[64,64,128]{2,1,0:T(8,128)(2,1)}, u32[]{:S(2)}, u32[]{:S(2)}) async-start(bf16[64,64,128]{2,1,0:T(8,128)(2,1)} %get-tuple-element.14.sent_ref), calls=%async_computation.2 | async-start | bytes 2097152 | tf_op jit(solution)/shard_map/all_to_all | solution.py:231
  93.9 0.6 add_add_fusion.fock_ref
  94.6 3.4 %local.1 = (f32[28,128,128]{2,1,0:T(8,128)}, f32[8,128]{1,0:T(8,128)S(1)}) custom-call(s32[28]{0:T(128)S(1)} %xor_convert_fusion.lead_ref, s32[28]{0:T(128)S(1)} %get-tuple-element.22.target_ref, f32[28]{0:T(128)S(1)} %add_add_fusion.fock_ref, bf16[28,128,128]{2,1,0:T(8,128)(2,1)S(1)} %copy-done, bf16[28,128,128]{2,1,0:T(8,128)(2,1)S(1)} %copy-done.4, ...), custom_call_target="tpu_custom_call" | custom-call | flops 2752512 | bytes 3670016 | tf_op jit(solution)/shard_map/local/pallas_call | solution.py:199
  98.0 7.3 %collective-permute-start.8 = (f32[8,128]{1,0:T(8,128)S(1)}, f32[8,128]{1,0:T(8,128)S(1)}, u32[]{:S(2)}, u32[]{:S(2)}) collective-permute-start(f32[8,128]{1,0:T(8,128)S(1)} %add.107), channel_id=1, source_target_pairs={{0,32},{1,33},{2,34},{3,35},{4,36},{5,37},{6,38},{7,39},{8,40},{9,... | collective-permute-start | bytes 12296 | tf_op jit(solution)/shard_map/ppermute | solution.py:217
  105.3 2.1 %collective-permute-start.9 = (f32[8,128]{1,0:T(8,128)S(1)}, f32[8,128]{1,0:T(8,128)S(1)}, u32[]{:S(2)}, u32[]{:S(2)}) collective-permute-start(f32[8,128]{1,0:T(8,128)S(1)} %add.107), channel_id=1, source_target_pairs={{0,48},{1,49},{2,50},{3,51},{4,52},{5,53},{6,54},{7,55},{8,56},{9,... | collective-permute-start | bytes 12296 | tf_op jit(solution)/shard_map/ppermute | solution.py:217
  107.4 2.1 %collective-permute-start.7 = (f32[8,128]{1,0:T(8,128)S(1)}, f32[8,128]{1,0:T(8,128)S(1)}, u32[]{:S(2)}, u32[]{:S(2)}) collective-permute-start(f32[8,128]{1,0:T(8,128)S(1)} %add.107), channel_id=1, source_target_pairs={{0,16},{1,17},{2,18},{3,19},{4,20},{5,21},{6,22},{7,23},{8,24},{9,... | collective-permute-start | bytes 12296 | tf_op jit(solution)/shard_map/ppermute | solution.py:217
  109.5 11.1 %collective-permute-done.8 = f32[8,128]{1,0:T(8,128)S(1)} collective-permute-done((f32[8,128]{1,0:T(8,128)S(1)}, f32[8,128]{1,0:T(8,128)S(1)}, u32[]{:S(2)}, u32[]{:S(2)}) %collective-permute-start.8) | collective-permute-done | bytes 4128 | tf_op jit(solution)/shard_map/ppermute | solution.py:217
  121.3 4.0 %join.1 = bf16[28,128,128]{2,1,0:T(8,128)(2,1)} custom-call(s32[28]{0:T(128)S(1)} %xor_convert_fusion.lead_ref, s32[28]{0:T(128)S(1)} %get-tuple-element.22.target_ref, f32[28]{0:T(128)S(1)} %add_multiply_fusion.shift_ref, bf16[64,64,128]{2,1,0:T(8,128)(2,1)} %all-to-all-done.2.returned_ref, f32[28,128,128]{2,1,0:T(8,128)} %get-tuple-element.16.local_ref, ...), custom_call_target="tpu_custom_call" | custom-call | flops 458752 | bytes 2883584 | tf_op jit(solution)/shard_map/join/pallas_call | solution.py:199
  (54 shorter events, 3.8 us)
Async XLA Ops:
  1.3 20.9 %all-to-all-start = ((s32[64,1,128]{2,1,0:T(1,128)}), s32[64,1,128]{2,1,0:T(1,128)S(1)}, u32[]{:S(2)}, u32[]{:S(2)}) async-start(s32[64,1,128]{2,1,0:T(1,128)} %pad.12), calls=%async_computation | async-start | bytes 65536 | tf_op jit(solution)/shard_map/all_to_all | solution.py:231
  12.9 0.7 copy-start.6
  13.6 8.7 %copy-start.1 = (bf16[48,128,128]{2,1,0:T(8,128)(2,1)S(1)}, bf16[48,128,128]{2,1,0:T(8,128)(2,1)}, u32[]{:S(2)}) copy-start(bf16[48,128,128]{2,1,0:T(8,128)(2,1)} %margin_ref.3) | copy-start | bytes 4718596
  13.6 8.7 %copy-start.5 = (s32[3072]{0:T(1024)S(1)}, s32[3072]{0:T(1024)}, u32[]{:S(2)}) copy-start(s32[3072]{0:T(1024)} %dst_ref.1) | copy-start | bytes 36868
  13.6 8.7 %copy-start.7 = (f32[48]{0:T(128)S(1)}, f32[48]{0:T(128)}, u32[]{:S(2)}) copy-start(f32[48]{0:T(128)} %fock_ref.1) | copy-start | bytes 580
  26.8 5.4 %copy-start.9 = (f32[1000]{0:T(1024)S(1)}, f32[1000]{0:T(1024)}, u32[]{:S(2)}) copy-start(f32[1000]{0:T(1024)} %param.13) | copy-start | bytes 12004
  26.8 5.4 %copy-start = (bf16[28,128,128]{2,1,0:T(8,128)(2,1)S(1)}, bf16[28,128,128]{2,1,0:T(8,128)(2,1)}, u32[]{:S(2)}) copy-start(bf16[28,128,128]{2,1,0:T(8,128)(2,1)} %amps_ref.7) | copy-start | bytes 2752516
  26.8 55.1 %all-to-all-start.1 = ((bf16[64,128,128]{2,1,0:T(8,128)(2,1)}), bf16[64,128,128]{2,1,0:T(8,128)(2,1)S(1)}, u32[]{:S(2)}, u32[]{:S(2)}) async-start(bf16[64,128,128]{2,1,0:T(8,128)(2,1)} %couple.1), calls=%async_computation.1 | async-start | bytes 4194304 | tf_op jit(solution)/shard_map/all_to_all | solution.py:231
  32.2 2.4 %copy-start.10 = (s32[2,28]{1,0:T(2,128)S(1)}, s32[2,28]{1,0:T(2,128)}, u32[]{:S(2)}) copy-start(s32[2,28]{1,0:T(2,128)} %param.14) | copy-start | bytes 676
  32.2 13.7 %copy-start.11 = (s32[28]{0:T(128)S(1)}, s32[28]{0:T(128)}, u32[]{:S(2)}) copy-start(s32[28]{0:T(128)} %param.15) | copy-start | bytes 340
  32.3 1.2 copy-start.3
  34.8 5.3 %collective-permute-start = (f32[8,128]{1,0:T(8,128)S(1)}, f32[8,128]{1,0:T(8,128)S(1)}, u32[]{:S(2)}, u32[]{:S(2)}) collective-permute-start(f32[8,128]{1,0:T(8,128)S(1)} %bitcast.13), channel_id=1, source_target_pairs={{0,64},{64,0},{128,192},{192,128},{256,320},{320,256},{384,448},{4... | collective-permute-start | bytes 12296 | tf_op jit(solution)/shard_map/ppermute | solution.py:217
  40.1 6.8 %collective-permute-start.1 = (f32[8,128]{1,0:T(8,128)S(1)}, f32[8,128]{1,0:T(8,128)S(1)}, u32[]{:S(2)}, u32[]{:S(2)}) collective-permute-start(f32[8,128]{1,0:T(8,128)S(1)} %bitcast_add_fusion), channel_id=1, source_target_pairs={{0,128},{64,192},{128,0},{192,64},{256,384},{320,448},{384,256},{4... | collective-permute-start | bytes 12296 | tf_op jit(solution)/shard_map/ppermute | solution.py:217
  46.9 10.0 %collective-permute-start.2 = (f32[8,128]{1,0:T(8,128)S(1)}, f32[8,128]{1,0:T(8,128)S(1)}, u32[]{:S(2)}, u32[]{:S(2)}) collective-permute-start(f32[8,128]{1,0:T(8,128)S(1)} %fusion.6), channel_id=1, source_target_pairs={{0,256},{64,320},{128,384},{192,448},{256,0},{320,64},{384,128},{4... | collective-permute-start | bytes 12296 | tf_op jit(solution)/shard_map/ppermute | solution.py:217
  56.9 5.4 %collective-permute-start.3 = (f32[8,128]{1,0:T(8,128)S(1)}, f32[8,128]{1,0:T(8,128)S(1)}, u32[]{:S(2)}, u32[]{:S(2)}) collective-permute-start(f32[8,128]{1,0:T(8,128)S(1)} %add.96), channel_id=1, source_target_pairs={{0,1},{1,0},{2,3},{3,2},{4,5},{5,4},{6,7},{7,6},{8,9},{9,8},{10,11... | collective-permute-start | bytes 12296 | tf_op jit(solution)/shard_map/ppermute | solution.py:217
  62.4 4.6 %collective-permute-start.4 = (f32[8,128]{1,0:T(8,128)S(1)}, f32[8,128]{1,0:T(8,128)S(1)}, u32[]{:S(2)}, u32[]{:S(2)}) collective-permute-start(f32[8,128]{1,0:T(8,128)S(1)} %add.97), channel_id=1, source_target_pairs={{0,2},{1,3},{2,0},{3,1},{4,6},{5,7},{6,4},{7,5},{8,10},{9,11},{10,... | collective-permute-start | bytes 12296 | tf_op jit(solution)/shard_map/ppermute | solution.py:217
  67.0 6.2 %collective-permute-start.5 = (f32[8,128]{1,0:T(8,128)S(1)}, f32[8,128]{1,0:T(8,128)S(1)}, u32[]{:S(2)}, u32[]{:S(2)}) collective-permute-start(f32[8,128]{1,0:T(8,128)S(1)} %add.98), channel_id=1, source_target_pairs={{0,4},{1,5},{2,6},{3,7},{4,0},{5,1},{6,2},{7,3},{8,12},{9,13},{10,... | collective-permute-start | bytes 12296 | tf_op jit(solution)/shard_map/ppermute | solution.py:217
  73.3 5.6 %collective-permute-start.6 = (f32[8,128]{1,0:T(8,128)S(1)}, f32[8,128]{1,0:T(8,128)S(1)}, u32[]{:S(2)}, u32[]{:S(2)}) collective-permute-start(f32[8,128]{1,0:T(8,128)S(1)} %add.99), channel_id=1, source_target_pairs={{0,8},{1,9},{2,10},{3,11},{4,12},{5,13},{6,14},{7,15},{8,0},{9,1},... | collective-permute-start | bytes 12296 | tf_op jit(solution)/shard_map/ppermute | solution.py:217
  81.9 11.4 %copy-start.8 = (f32[28,128]{1,0:T(8,128)S(1)}, f32[28,128]{1,0:T(8,128)}, u32[]{:S(2)}) copy-start(f32[28,128]{1,0:T(8,128)} %param.12) | copy-start | bytes 43012
  84.1 10.5 %copy-start.2 = (bf16[64,64,128]{2,1,0:T(8,128)(2,1)S(1)}, bf16[64,64,128]{2,1,0:T(8,128)(2,1)}, u32[]{:S(2)}) copy-start(bf16[64,64,128]{2,1,0:T(8,128)(2,1)} %get-tuple-element.14.sent_ref) | copy-start | bytes 3145732
  84.1 10.5 %copy-start.4 = (bf16[28,128,128]{2,1,0:T(8,128)(2,1)S(1)}, bf16[28,128,128]{2,1,0:T(8,128)(2,1)}, u32[]{:S(2)}) copy-start(bf16[28,128,128]{2,1,0:T(8,128)(2,1)} %ints_ref.3) | copy-start | bytes 2752516
  84.1 37.2 %all-to-all-start.2 = ((bf16[64,64,128]{2,1,0:T(8,128)(2,1)}), bf16[64,64,128]{2,1,0:T(8,128)(2,1)}, u32[]{:S(2)}, u32[]{:S(2)}) async-start(bf16[64,64,128]{2,1,0:T(8,128)(2,1)} %get-tuple-element.14.sent_ref), calls=%async_computation.2 | async-start | bytes 2097152 | tf_op jit(solution)/shard_map/all_to_all | solution.py:231
  98.0 22.6 %collective-permute-start.8 = (f32[8,128]{1,0:T(8,128)S(1)}, f32[8,128]{1,0:T(8,128)S(1)}, u32[]{:S(2)}, u32[]{:S(2)}) collective-permute-start(f32[8,128]{1,0:T(8,128)S(1)} %add.107), channel_id=1, source_target_pairs={{0,32},{1,33},{2,34},{3,35},{4,36},{5,37},{6,38},{7,39},{8,40},{9,... | collective-permute-start | bytes 12296 | tf_op jit(solution)/shard_map/ppermute | solution.py:217
  105.3 15.3 %collective-permute-start.9 = (f32[8,128]{1,0:T(8,128)S(1)}, f32[8,128]{1,0:T(8,128)S(1)}, u32[]{:S(2)}, u32[]{:S(2)}) collective-permute-start(f32[8,128]{1,0:T(8,128)S(1)} %add.107), channel_id=1, source_target_pairs={{0,48},{1,49},{2,50},{3,51},{4,52},{5,53},{6,54},{7,55},{8,56},{9,... | collective-permute-start | bytes 12296 | tf_op jit(solution)/shard_map/ppermute | solution.py:217
  107.4 13.2 %collective-permute-start.7 = (f32[8,128]{1,0:T(8,128)S(1)}, f32[8,128]{1,0:T(8,128)S(1)}, u32[]{:S(2)}, u32[]{:S(2)}) collective-permute-start(f32[8,128]{1,0:T(8,128)S(1)} %add.107), channel_id=1, source_target_pairs={{0,16},{1,17},{2,18},{3,19},{4,20},{5,21},{6,22},{7,23},{8,24},{9,... | collective-permute-start | bytes 12296 | tf_op jit(solution)/shard_map/ppermute | solution.py:217

commit v5 on v4

--- a/solution.py
+++ b/solution.py
@@ -149,7 +149,7 @@
 
 
 def join_kernel(lead_ref, target_ref, shift_ref, returned_ref, local_ref, amps_ref, out_ref, tiles, locals_, results, sems, in_sems, out_sems):
-    pairs, half, rank = tiles.shape
+    pairs, _, rank = tiles.shape
     chunks = in_sems.shape[0]
     count = pairs // chunks
     one = unit(rank)
@@ -195,14 +195,13 @@
 HBM = pl.BlockSpec(memory_space=pltpu.HBM)
 
 
-def call(kernel, name, scalars, arrays, out_shape, out_specs, flops, nbytes, scratch=(), specs=None):
+def call(kernel, scalars, arrays, out_shape, out_specs, flops, nbytes, scratch=(), specs=None):
     return pl.pallas_call(
         kernel,
         in_specs=[SMEM] * len(scalars) + (specs or [VMEM] * len(arrays)),
         out_specs=out_specs,
         out_shape=out_shape,
         scratch_shapes=scratch,
-        name=name,
         cost_estimate=pl.CostEstimate(flops=flops, bytes_accessed=nbytes, transcendentals=0),
         compiler_params=pltpu.CompilerParams(vmem_limit_bytes=KERNEL_VMEM),
     )(*scalars, *arrays)
@@ -231,7 +230,7 @@
     return lax.all_to_all(tiles, "own", split_axis=0, concat_axis=0, tiled=True)
 
 
-def local(
+def local_part(
     amps, ints, pno_energy, occ_energy, pair_occ, mirror, edge_src, edge_dst, edge_fock, margin
 ):
     owners = lax.axis_size("own")
@@ -255,7 +254,6 @@
 
     projected = call(
         project_kernel,
-        "project",
         [edge_src],
         [
             pltpu.with_memory_space_constraint(margin, pltpu.HBM),
@@ -277,7 +275,6 @@
     group_dst = edge_dst - group_base
     outgoing = call(
         functools.partial(couple_kernel, pairs),
-        "couple",
         [table, edge_dst, edge_fock],
         [projected, margin],
         pltpu.HBM((owners, rank, rank), BF16),
@@ -290,7 +287,6 @@
 
     lane_energy = call(
         energy_kernel,
-        "energy",
         [],
         [amps, ints],
         jax.ShapeDtypeStruct((pairs, 1, rank), F32),
@@ -307,7 +303,8 @@
     total = partial_value.reshape(padded // LANES, LANES)
     own_steps = powers(owners)
     total = all_sum(total, "grp", powers(groups))
-    total = all_sum(total, "own", own_steps[:-2])
+    total = all_sum(total, "own", own_steps[:-3])
+    late = swapped(total, "own", own_steps[-3])
     occ_wide = jnp.pad(occ_energy, (0, padded - occ_count))
     fock_pair = pick_rows(occ_wide, first_hit) + pick_rows(occ_wide, second_hit)
 
@@ -322,11 +319,9 @@
     direct_row = jnp.where(direct_row == 0, pairs, direct_row - 1)
     turned_row = jnp.where(turned_row == 0, pairs, turned_row - 1)
 
-    total, direct_row = lax.optimization_barrier((total, direct_row))
 
     sent, mark = call(
         sum_kernel,
-        "sum",
         [direct_row, turned_row, mirror_owner],
         [arrived],
         [pltpu.HBM((owners, half, rank), BF16), jax.ShapeDtypeStruct((8, LANES), F32)],
@@ -345,7 +340,6 @@
 
     twice_local, done = call(
         local_kernel,
-        "local",
         [lead, mirror_owner, fock_pair],
         [amps, ints, pno_energy.reshape(pairs, 1, rank), sent],
         [pltpu.HBM((pairs, rank, rank), F32), jax.ShapeDtypeStruct((8, LANES), F32)],
@@ -354,7 +348,7 @@
         4 * pairs * tile_bytes,
         [pltpu.VMEM((pairs, rank, rank), F32), pltpu.SemaphoreType.DMA],
     )
-    total = total + done
+    total = total + late + done
     low, high = own_steps[-2:]
     moved = [swapped(total, "own", step) for step in (low, high, low + high)]
     total = total + moved[0] + (moved[1] + moved[2])
@@ -362,7 +356,6 @@
     shift = 0.5 * (pick_rows(occ_sums, first_hit) + pick_rows(occ_sums, second_hit))
     return call(
         join_kernel,
-        "join",
         [lead, mirror_owner, shift],
         [
             pltpu.with_memory_space_constraint(returned, pltpu.HBM),
@@ -378,8 +371,8 @@
             pltpu.VMEM((pairs, rank, rank), F32),
             pltpu.VMEM((pairs, rank, rank), BF16),
             pltpu.SemaphoreType.DMA((pairs,)),
-            pltpu.SemaphoreType.DMA((7,)),
-            pltpu.SemaphoreType.DMA((7,)),
+            pltpu.SemaphoreType.DMA((4,)),
+            pltpu.SemaphoreType.DMA((4,)),
         ],
         [HBM, HBM, VMEM],
     )
@@ -399,4 +392,4 @@
         P(("grp", "own"), None, None),
     )
     out_specs = P(("grp", "own"), None, None)
-    return jax.shard_map(local, mesh=mesh, in_specs=in_specs, out_specs=out_specs, check_vma=False)
+    return jax.shard_map(local_part, mesh=mesh, in_specs=in_specs, out_specs=out_specs, check_vma=False)

time: 126 us -> 161 us (1.28)
  the two profiles are of different devices: /device:TPU:1 before, /device:TPU:2 now
where the time goes in v5:
time: 161 us; the launch traced here: 160 us
  waiting for transfers between devices  70.8 us (44%)
  starting transfers between devices  65.9 us (41%)
  Pallas kernels  18.3 us (11%)
  local copies, waits for them, and re-layouts  2.67 us (2%)
  other arithmetic  1.9 us (1%)
    all_to_all x3, waiting for transfers between devices, exchange(): return lax.all_to_all(tiles, 'own', split_axis=0, concat_axis=0, tiled=True)  54.9 us
    ppermute x10, starting transfers between devices, swapped(): return lax.ppermute(value, axis, [(i, i ^ step) for i in range(members)])  43.5 us
    all_to_all x3, starting transfers between devices, exchange(): return lax.all_to_all(tiles, 'own', split_axis=0, concat_axis=0, tiled=True)  22.4 us
    pallas_call x6, Pallas kernels, call(): pl.pallas_call(kernel, in_specs=[SMEM] * len(scalars) + (specs or [VMEM]...  18.3 us
    ppermute x10, waiting for transfers between devices, swapped(): return lax.ppermute(value, axis, [(i, i ^ step) for i in range(members)])  15.8 us
  transfers between devices with their start and end apart: 13, of which 10 were waited for; matrix products, arithmetic and copies ran while one was open for 2% of the time, Pallas kernels for 5%

profile of v5, /device:TPU:2, one launch (start us, length us, event | category | flops | bytes accessed | tf_op | source)
XLA Modules:
  0.0 159.9 jit_solution(6353705775833877561)
XLA Ops:
  0.0 0.7 pad.11
  1.3 10.7 %all-to-all-start = ((s32[64,1,128]{2,1,0:T(1,128)}), s32[64,1,128]{2,1,0:T(1,128)S(1)}, u32[]{:S(2)}, u32[]{:S(2)}) async-start(s32[64,1,128]{2,1,0:T(1,128)} %pad.12), calls=%async_computation | async-start | bytes 65536 | tf_op jit(solution)/shard_map/all_to_all | solution.py:230
  12.0 0.6 copy-done.5
  12.6 3.5 %shard_map.101.proj_ref = bf16[48,128,128]{2,1,0:T(8,128)(2,1)S(1)} custom-call(s32[48]{0:T(128)S(1)} %copy-done.5, bf16[48,128,128]{2,1,0:T(8,128)(2,1)} %margin_ref.3, bf16[28,128,128]{2,1,0:T(8,128)(2,1)} %amps_ref.7), custom_call_target="tpu_custom_call" | custom-call | flops 201326592 | bytes 4063232 | tf_op jit(solution)/shard_map/pallas_call | solution.py:199
  16.2 4.3 %all-to-all-done = s32[64,1,128]{2,1,0:T(1,128)S(1)} async-done(((s32[64,1,128]{2,1,0:T(1,128)}), s32[64,1,128]{2,1,0:T(1,128)S(1)}, u32[]{:S(2)}, u32[]{:S(2)}) %all-to-all-start) | async-done | bytes 32800 | tf_op jit(solution)/shard_map/all_to_all | solution.py:230
  20.5 4.6 %shard_map.102 = bf16[64,128,128]{2,1,0:T(8,128)(2,1)} custom-call(s32[8192]{0:T(1024)S(1)} %bitcast.12, s32[3072]{0:T(1024)S(1)} %copy-done.4, f32[48]{0:T(128)S(1)} %copy-done.6, bf16[48,128,128]{2,1,0:T(8,128)(2,1)S(1)} %shard_map.101.proj_ref, bf16[48,128,128]{2,1,0:T(8,128)(2,1)S(1)} %copy-done.1), custom_call_target="tpu_custom_call" | custom-call | flops 201326592 | bytes 4718592 | tf_op jit(solution)/shard_map/pallas_call | solution.py:199
  25.1 6.0 %all-to-all-start.1 = ((bf16[64,128,128]{2,1,0:T(8,128)(2,1)}), bf16[64,128,128]{2,1,0:T(8,128)(2,1)S(1)}, u32[]{:S(2)}, u32[]{:S(2)}) async-start(bf16[64,128,128]{2,1,0:T(8,128)(2,1)} %shard_map.102), calls=%async_computation.1 | async-start | bytes 4194304 | tf_op jit(solution)/shard_map/all_to_all | solution.py:230
  31.8 50.6 %all-to-all-done.1.arrived_ref = bf16[64,128,128]{2,1,0:T(8,128)(2,1)S(1)} async-done(((bf16[64,128,128]{2,1,0:T(8,128)(2,1)}), bf16[64,128,128]{2,1,0:T(8,128)(2,1)S(1)}, u32[]{:S(2)}, u32[]{:S(2)}) %all-to-all-start.1) | async-done | bytes 2097184 | tf_op jit(solution)/shard_map/all_to_all | solution.py:230
  82.3 2.2 %shard_map.103 = (bf16[64,64,128]{2,1,0:T(8,128)(2,1)}, f32[8,128]{1,0:T(8,128)S(1)}) custom-call(s32[64]{0:T(128)S(1)} %get-tuple-element.23.direct_ref, s32[64]{0:T(128)S(1)} %get-tuple-element.22.turned_ref, s32[28]{0:T(128)S(1)} %get-tuple-element.18.target_ref, bf16[64,128,128]{2,1,0:T(8,128)(2,1)S(1)} %all-to-all-done.1.arrived_ref), custom_call_target="tpu_custom_call" | custom-call | flops 4194304 | bytes 3014656 | tf_op jit(solution)/shard_map/pallas_call | solution.py:199
  84.6 5.8 %all-to-all-start.2 = ((bf16[64,64,128]{2,1,0:T(8,128)(2,1)}), bf16[64,64,128]{2,1,0:T(8,128)(2,1)}, u32[]{:S(2)}, u32[]{:S(2)}) async-start(bf16[64,64,128]{2,1,0:T(8,128)(2,1)} %get-tuple-element.10.sent_ref), calls=%async_computation.2 | async-start | bytes 2097152 | tf_op jit(solution)/shard_map/all_to_all | solution.py:230
  90.4 0.9 shard_map.100
  91.8 4.3 %collective-permute-start = (f32[8,128]{1,0:T(8,128)S(1)}, f32[8,128]{1,0:T(8,128)S(1)}, u32[]{:S(2)}, u32[]{:S(2)}) collective-permute-start(f32[8,128]{1,0:T(8,128)S(1)} %bitcast.13), channel_id=1, source_target_pairs={{0,64},{64,0},{128,192},{192,128},{256,320},{320,256},{384,448},{4... | collective-permute-start | bytes 12296 | tf_op jit(solution)/shard_map/ppermute | solution.py:216
  96.1 1.6 collective-permute-done
  97.6 6.1 %collective-permute-start.1 = (f32[8,128]{1,0:T(8,128)S(1)}, f32[8,128]{1,0:T(8,128)S(1)}, u32[]{:S(2)}, u32[]{:S(2)}) collective-permute-start(f32[8,128]{1,0:T(8,128)S(1)} %bitcast_add_fusion), channel_id=1, source_target_pairs={{0,128},{64,192},{128,0},{192,64},{256,384},{320,448},{384,256},{4... | collective-permute-start | bytes 12296 | tf_op jit(solution)/shard_map/ppermute | solution.py:216
  103.7 1.6 collective-permute-done.1
  105.3 9.3 %collective-permute-start.2 = (f32[8,128]{1,0:T(8,128)S(1)}, f32[8,128]{1,0:T(8,128)S(1)}, u32[]{:S(2)}, u32[]{:S(2)}) collective-permute-start(f32[8,128]{1,0:T(8,128)S(1)} %fusion.6), channel_id=1, source_target_pairs={{0,256},{64,320},{128,384},{192,448},{256,0},{320,64},{384,128},{4... | collective-permute-start | bytes 12296 | tf_op jit(solution)/shard_map/ppermute | solution.py:216
  114.6 1.6 collective-permute-done.2
  116.2 1.9 %collective-permute-start.3 = (f32[8,128]{1,0:T(8,128)S(1)}, f32[8,128]{1,0:T(8,128)S(1)}, u32[]{:S(2)}, u32[]{:S(2)}) collective-permute-start(f32[8,128]{1,0:T(8,128)S(1)} %add.96), channel_id=1, source_target_pairs={{0,1},{1,0},{2,3},{3,2},{4,5},{5,4},{6,7},{7,6},{8,9},{9,8},{10,11... | collective-permute-start | bytes 12296 | tf_op jit(solution)/shard_map/ppermute | solution.py:216
  118.1 1.1 collective-permute-done.3
  119.2 2.4 %collective-permute-start.4 = (f32[8,128]{1,0:T(8,128)S(1)}, f32[8,128]{1,0:T(8,128)S(1)}, u32[]{:S(2)}, u32[]{:S(2)}) collective-permute-start(f32[8,128]{1,0:T(8,128)S(1)} %add.97), channel_id=1, source_target_pairs={{0,2},{1,3},{2,0},{3,1},{4,6},{5,7},{6,4},{7,5},{8,10},{9,11},{10,... | collective-permute-start | bytes 12296 | tf_op jit(solution)/shard_map/ppermute | solution.py:216
  121.6 3.0 %collective-permute-done.4 = f32[8,128]{1,0:T(8,128)S(1)} collective-permute-done((f32[8,128]{1,0:T(8,128)S(1)}, f32[8,128]{1,0:T(8,128)S(1)}, u32[]{:S(2)}, u32[]{:S(2)}) %collective-permute-start.4) | collective-permute-done | bytes 4128 | tf_op jit(solution)/shard_map/ppermute | solution.py:216
  124.7 4.0 %collective-permute-start.5 = (f32[8,128]{1,0:T(8,128)S(1)}, f32[8,128]{1,0:T(8,128)S(1)}, u32[]{:S(2)}, u32[]{:S(2)}) collective-permute-start(f32[8,128]{1,0:T(8,128)S(1)} %add.98), channel_id=1, source_target_pairs={{0,4},{1,5},{2,6},{3,7},{4,0},{5,1},{6,2},{7,3},{8,12},{9,13},{10,... | collective-permute-start | bytes 12296 | tf_op jit(solution)/shard_map/ppermute | solution.py:216
  128.7 3.0 %collective-permute-done.5 = f32[8,128]{1,0:T(8,128)S(1)} collective-permute-done((f32[8,128]{1,0:T(8,128)S(1)}, f32[8,128]{1,0:T(8,128)S(1)}, u32[]{:S(2)}, u32[]{:S(2)}) %collective-permute-start.5) | collective-permute-done | bytes 4128 | tf_op jit(solution)/shard_map/ppermute | solution.py:216
  131.7 3.4 %collective-permute-start.6 = (f32[8,128]{1,0:T(8,128)S(1)}, f32[8,128]{1,0:T(8,128)S(1)}, u32[]{:S(2)}, u32[]{:S(2)}) collective-permute-start(f32[8,128]{1,0:T(8,128)S(1)} %add.99), channel_id=1, source_target_pairs={{0,8},{1,9},{2,10},{3,11},{4,12},{5,13},{6,14},{7,15},{8,0},{9,1},... | collective-permute-start | bytes 12296 | tf_op jit(solution)/shard_map/ppermute | solution.py:216
  135.6 0.6 add_add_fusion.1.fock_ref
  136.2 3.4 %shard_map.104 = (f32[28,128,128]{2,1,0:T(8,128)}, f32[8,128]{1,0:T(8,128)S(1)}) custom-call(s32[28]{0:T(128)S(1)} %xor_convert_fusion.lead_ref, s32[28]{0:T(128)S(1)} %get-tuple-element.18.target_ref, f32[28]{0:T(128)S(1)} %add_add_fusion.1.fock_ref, bf16[28,128,128]{2,1,0:T(8,128)(2,1)S(1)} %copy-done, bf16[28,128,128]{2,1,0:T(8,128)(2,1)S(1)} %copy-done.3, ...), custom_call_target="tpu_custom_call" | custom-call | flops 2752512 | bytes 3670016 | tf_op jit(solution)/shard_map/pallas_call | solution.py:199
  139.7 6.5 %collective-permute-start.8 = (f32[8,128]{1,0:T(8,128)S(1)}, f32[8,128]{1,0:T(8,128)S(1)}, u32[]{:S(2)}, u32[]{:S(2)}) collective-permute-start(f32[8,128]{1,0:T(8,128)S(1)} %add_add_fusion), channel_id=1, source_target_pairs={{0,32},{1,33},{2,34},{3,35},{4,36},{5,37},{6,38},{7,39},{8,40},{9,... | collective-permute-start | bytes 12296 | tf_op jit(solution)/shard_map/ppermute | solution.py:216
  146.2 3.3 %collective-permute-start.9 = (f32[8,128]{1,0:T(8,128)S(1)}, f32[8,128]{1,0:T(8,128)S(1)}, u32[]{:S(2)}, u32[]{:S(2)}) collective-permute-start(f32[8,128]{1,0:T(8,128)S(1)} %add_add_fusion), channel_id=1, source_target_pairs={{0,48},{1,49},{2,50},{3,51},{4,52},{5,53},{6,54},{7,55},{8,56},{9,... | collective-permute-start | bytes 12296 | tf_op jit(solution)/shard_map/ppermute | solution.py:216
  149.5 2.4 %collective-permute-start.7 = (f32[8,128]{1,0:T(8,128)S(1)}, f32[8,128]{1,0:T(8,128)S(1)}, u32[]{:S(2)}, u32[]{:S(2)}) collective-permute-start(f32[8,128]{1,0:T(8,128)S(1)} %add_add_fusion), channel_id=1, source_target_pairs={{0,16},{1,17},{2,18},{3,19},{4,20},{5,21},{6,22},{7,23},{8,24},{9,... | collective-permute-start | bytes 12296 | tf_op jit(solution)/shard_map/ppermute | solution.py:216
  151.9 1.9 %collective-permute-done.9 = f32[8,128]{1,0:T(8,128)S(1)} collective-permute-done((f32[8,128]{1,0:T(8,128)S(1)}, f32[8,128]{1,0:T(8,128)S(1)}, u32[]{:S(2)}, u32[]{:S(2)}) %collective-permute-start.9) | collective-permute-done | bytes 4128 | tf_op jit(solution)/shard_map/ppermute | solution.py:216
  153.9 2.1 %collective-permute-done.7 = f32[8,128]{1,0:T(8,128)S(1)} collective-permute-done((f32[8,128]{1,0:T(8,128)S(1)}, f32[8,128]{1,0:T(8,128)S(1)}, u32[]{:S(2)}, u32[]{:S(2)}) %collective-permute-start.7) | collective-permute-done | bytes 4128 | tf_op jit(solution)/shard_map/ppermute | solution.py:216
  156.1 3.7 %shard_map.105 = bf16[28,128,128]{2,1,0:T(8,128)(2,1)} custom-call(s32[28]{0:T(128)S(1)} %xor_convert_fusion.lead_ref, s32[28]{0:T(128)S(1)} %get-tuple-element.18.target_ref, f32[28]{0:T(128)S(1)} %add_multiply_fusion.shift_ref, bf16[64,64,128]{2,1,0:T(8,128)(2,1)} %all-to-all-done.2.returned_ref, f32[28,128,128]{2,1,0:T(8,128)} %get-tuple-element.12.local_ref, ...), custom_call_target="tpu_custom_call" | custom-call | flops 458752 | bytes 2883584 | tf_op jit(solution)/shard_map/pallas_call | solution.py:199
  (50 shorter events, 2.6 us)
Async XLA Ops:
  1.3 19.2 %all-to-all-start = ((s32[64,1,128]{2,1,0:T(1,128)}), s32[64,1,128]{2,1,0:T(1,128)S(1)}, u32[]{:S(2)}, u32[]{:S(2)}) async-start(s32[64,1,128]{2,1,0:T(1,128)} %pad.12), calls=%async_computation | async-start | bytes 65536 | tf_op jit(solution)/shard_map/all_to_all | solution.py:230
  12.0 0.7 copy-start.5
  12.6 7.9 %copy-start.1 = (bf16[48,128,128]{2,1,0:T(8,128)(2,1)S(1)}, bf16[48,128,128]{2,1,0:T(8,128)(2,1)}, u32[]{:S(2)}) copy-start(bf16[48,128,128]{2,1,0:T(8,128)(2,1)} %margin_ref.3) | copy-start | bytes 4718596
  12.6 7.9 %copy-start.4 = (s32[3072]{0:T(1024)S(1)}, s32[3072]{0:T(1024)}, u32[]{:S(2)}) copy-start(s32[3072]{0:T(1024)} %dst_ref.1) | copy-start | bytes 36868
  12.6 7.9 %copy-start.6 = (f32[48]{0:T(128)S(1)}, f32[48]{0:T(128)}, u32[]{:S(2)}) copy-start(f32[48]{0:T(128)} %fock_ref.1) | copy-start | bytes 580
  25.1 6.3 %copy-start.10 = (s32[28]{0:T(128)S(1)}, s32[28]{0:T(128)}, u32[]{:S(2)}) copy-start(s32[28]{0:T(128)} %param.15) | copy-start | bytes 340
  25.1 57.2 %all-to-all-start.1 = ((bf16[64,128,128]{2,1,0:T(8,128)(2,1)}), bf16[64,128,128]{2,1,0:T(8,128)(2,1)S(1)}, u32[]{:S(2)}, u32[]{:S(2)}) async-start(bf16[64,128,128]{2,1,0:T(8,128)(2,1)} %shard_map.102), calls=%async_computation.1 | async-start | bytes 4194304 | tf_op jit(solution)/shard_map/all_to_all | solution.py:230
  82.3 8.0 %copy-start.8 = (f32[1000]{0:T(1024)S(1)}, f32[1000]{0:T(1024)}, u32[]{:S(2)}) copy-start(f32[1000]{0:T(1024)} %param.13) | copy-start | bytes 12004
  82.3 8.1 %copy-start = (bf16[28,128,128]{2,1,0:T(8,128)(2,1)S(1)}, bf16[28,128,128]{2,1,0:T(8,128)(2,1)}, u32[]{:S(2)}) copy-start(bf16[28,128,128]{2,1,0:T(8,128)(2,1)} %amps_ref.7) | copy-start | bytes 2752516
  84.5 5.9 %copy-start.3 = (bf16[28,128,128]{2,1,0:T(8,128)(2,1)S(1)}, bf16[28,128,128]{2,1,0:T(8,128)(2,1)}, u32[]{:S(2)}) copy-start(bf16[28,128,128]{2,1,0:T(8,128)(2,1)} %ints_ref.3) | copy-start | bytes 2752516
  84.5 7.0 %copy-start.9 = (s32[2,28]{1,0:T(2,128)S(1)}, s32[2,28]{1,0:T(2,128)}, u32[]{:S(2)}) copy-start(s32[2,28]{1,0:T(2,128)} %param.14) | copy-start | bytes 676
  84.6 44.1 %copy-start.7 = (f32[28,128]{1,0:T(8,128)S(1)}, f32[28,128]{1,0:T(8,128)}, u32[]{:S(2)}) copy-start(f32[28,128]{1,0:T(8,128)} %param.12) | copy-start | bytes 43012
  84.6 51.7 %copy-start.2 = (bf16[64,64,128]{2,1,0:T(8,128)(2,1)S(1)}, bf16[64,64,128]{2,1,0:T(8,128)(2,1)}, u32[]{:S(2)}) copy-start(bf16[64,64,128]{2,1,0:T(8,128)(2,1)} %get-tuple-element.10.sent_ref) | copy-start | bytes 3145732
  84.6 71.6 %all-to-all-start.2 = ((bf16[64,64,128]{2,1,0:T(8,128)(2,1)}), bf16[64,64,128]{2,1,0:T(8,128)(2,1)}, u32[]{:S(2)}, u32[]{:S(2)}) async-start(bf16[64,64,128]{2,1,0:T(8,128)(2,1)} %get-tuple-element.10.sent_ref), calls=%async_computation.2 | async-start | bytes 2097152 | tf_op jit(solution)/shard_map/all_to_all | solution.py:230
  91.8 5.8 %collective-permute-start = (f32[8,128]{1,0:T(8,128)S(1)}, f32[8,128]{1,0:T(8,128)S(1)}, u32[]{:S(2)}, u32[]{:S(2)}) collective-permute-start(f32[8,128]{1,0:T(8,128)S(1)} %bitcast.13), channel_id=1, source_target_pairs={{0,64},{64,0},{128,192},{192,128},{256,320},{320,256},{384,448},{4... | collective-permute-start | bytes 12296 | tf_op jit(solution)/shard_map/ppermute | solution.py:216
  97.6 7.6 %collective-permute-start.1 = (f32[8,128]{1,0:T(8,128)S(1)}, f32[8,128]{1,0:T(8,128)S(1)}, u32[]{:S(2)}, u32[]{:S(2)}) collective-permute-start(f32[8,128]{1,0:T(8,128)S(1)} %bitcast_add_fusion), channel_id=1, source_target_pairs={{0,128},{64,192},{128,0},{192,64},{256,384},{320,448},{384,256},{4... | collective-permute-start | bytes 12296 | tf_op jit(solution)/shard_map/ppermute | solution.py:216
  105.3 10.8 %collective-permute-start.2 = (f32[8,128]{1,0:T(8,128)S(1)}, f32[8,128]{1,0:T(8,128)S(1)}, u32[]{:S(2)}, u32[]{:S(2)}) collective-permute-start(f32[8,128]{1,0:T(8,128)S(1)} %fusion.6), channel_id=1, source_target_pairs={{0,256},{64,320},{128,384},{192,448},{256,0},{320,64},{384,128},{4... | collective-permute-start | bytes 12296 | tf_op jit(solution)/shard_map/ppermute | solution.py:216
  116.2 3.0 %collective-permute-start.3 = (f32[8,128]{1,0:T(8,128)S(1)}, f32[8,128]{1,0:T(8,128)S(1)}, u32[]{:S(2)}, u32[]{:S(2)}) collective-permute-start(f32[8,128]{1,0:T(8,128)S(1)} %add.96), channel_id=1, source_target_pairs={{0,1},{1,0},{2,3},{3,2},{4,5},{5,4},{6,7},{7,6},{8,9},{9,8},{10,11... | collective-permute-start | bytes 12296 | tf_op jit(solution)/shard_map/ppermute | solution.py:216
  119.2 5.5 %collective-permute-start.4 = (f32[8,128]{1,0:T(8,128)S(1)}, f32[8,128]{1,0:T(8,128)S(1)}, u32[]{:S(2)}, u32[]{:S(2)}) collective-permute-start(f32[8,128]{1,0:T(8,128)S(1)} %add.97), channel_id=1, source_target_pairs={{0,2},{1,3},{2,0},{3,1},{4,6},{5,7},{6,4},{7,5},{8,10},{9,11},{10,... | collective-permute-start | bytes 12296 | tf_op jit(solution)/shard_map/ppermute | solution.py:216
  124.7 7.0 %collective-permute-start.5 = (f32[8,128]{1,0:T(8,128)S(1)}, f32[8,128]{1,0:T(8,128)S(1)}, u32[]{:S(2)}, u32[]{:S(2)}) collective-permute-start(f32[8,128]{1,0:T(8,128)S(1)} %add.98), channel_id=1, source_target_pairs={{0,4},{1,5},{2,6},{3,7},{4,0},{5,1},{6,2},{7,3},{8,12},{9,13},{10,... | collective-permute-start | bytes 12296 | tf_op jit(solution)/shard_map/ppermute | solution.py:216
  131.7 8.0 %collective-permute-start.6 = (f32[8,128]{1,0:T(8,128)S(1)}, f32[8,128]{1,0:T(8,128)S(1)}, u32[]{:S(2)}, u32[]{:S(2)}) collective-permute-start(f32[8,128]{1,0:T(8,128)S(1)} %add.99), channel_id=1, source_target_pairs={{0,8},{1,9},{2,10},{3,11},{4,12},{5,13},{6,14},{7,15},{8,0},{9,1},... | collective-permute-start | bytes 12296 | tf_op jit(solution)/shard_map/ppermute | solution.py:216
  139.7 12.2 %collective-permute-start.8 = (f32[8,128]{1,0:T(8,128)S(1)}, f32[8,128]{1,0:T(8,128)S(1)}, u32[]{:S(2)}, u32[]{:S(2)}) collective-permute-start(f32[8,128]{1,0:T(8,128)S(1)} %add_add_fusion), channel_id=1, source_target_pairs={{0,32},{1,33},{2,34},{3,35},{4,36},{5,37},{6,38},{7,39},{8,40},{9,... | collective-permute-start | bytes 12296 | tf_op jit(solution)/shard_map/ppermute | solution.py:216
  146.2 7.6 %collective-permute-start.9 = (f32[8,128]{1,0:T(8,128)S(1)}, f32[8,128]{1,0:T(8,128)S(1)}, u32[]{:S(2)}, u32[]{:S(2)}) collective-permute-start(f32[8,128]{1,0:T(8,128)S(1)} %add_add_fusion), channel_id=1, source_target_pairs={{0,48},{1,49},{2,50},{3,51},{4,52},{5,53},{6,54},{7,55},{8,56},{9,... | collective-permute-start | bytes 12296 | tf_op jit(solution)/shard_map/ppermute | solution.py:216
  149.5 6.4 %collective-permute-start.7 = (f32[8,128]{1,0:T(8,128)S(1)}, f32[8,128]{1,0:T(8,128)S(1)}, u32[]{:S(2)}, u32[]{:S(2)}) collective-permute-start(f32[8,128]{1,0:T(8,128)S(1)} %add_add_fusion), channel_id=1, source_target_pairs={{0,16},{1,17},{2,18},{3,19},{4,20},{5,21},{6,22},{7,23},{8,24},{9,... | collective-permute-start | bytes 12296 | tf_op jit(solution)/shard_map/ppermute | solution.py:216
